TPU v7x, 32 devices: a whole 2x2x4 slice. The times are simulated.
32 devices in a mesh: ens: 2 (over y), space: 4 (over z), tm: 2 (over x), spin: 2 (over core).
Axes of the slice: x: 2, y: 2, z: 4, core: 2. Of those that a mesh axis runs over, the one named last changes fastest.
Arguments:
- eigvecs: bfloat16 [4, 2, 3, 8192, 128], P('tm', None, None, 'space'), may hold values from -6 to 6
- links: bfloat16 [4, 3, 2, 3, 3, 8192], P('tm', None, None, None, None, 'space'), may hold values from -2.5 to 2.5
- directions: int32 [4], P('spin'), may hold values from 0 to 3, each once
- pair_list: int32 [32, 2], P(('space', 'tm')), may hold values from 0 to 3
- pair_operators: int32 [32, 2], P(('space', 'tm')), may hold values from 0 to 3
- perambulators: bfloat16 [32, 16, 2, 128, 128], P(('space', 'tm'), 'spin'), may hold values from -0.5 to 0.5
Outputs:
- elementals: float32 [8, 4, 128, 2, 128], P(('ens', 'tm'), 'spin', 'space'), parts along dimension 0
- correlators: float32 [64, 2], P(('ens', 'space', 'tm')), parts along dimension 0
There are 2 independent parts, one for each index of `ens`. A program takes and returns all parts, laid end to end along the dimension named above; an argument that names none is the same for every part. Nothing has to cross between parts.
Inputs may be any that keep to these rules, and one draw needn't show every extreme that they name: `directions`: each code once; 0, 1, 2 name a covariant derivative along the first, second and third spatial direction, 3 the eigenvectors with one unit of momentum along the third.
All inputs are finite; a program needn't handle non-finite values.
Results may differ from a plain program's by a relative error of at most 0.0071.
Values may be sent and summed in bfloat16 or wider, within the bound.
No kernel may reach another device: no remote copies, remote signals or barrier semaphores. Data moves between devices by JAX's collectives and lax.ppermute only.
A program may use at most 128 MiB of HBM per device.

v0:
```python
from functools import partial
import math

import jax
import jax.numpy as jnp
from jax import lax
from jax.sharding import PartitionSpec as P

PX = 16
PY = 16


def from_behind(array, axis, by):
    count = lax.axis_size(axis)
    return lax.ppermute(array, axis, [(i, (i + by) % count) for i in range(count)])


def apply_links(link_field, vectors):
    for b in range(3):
        link_real = link_field[0, :, b][..., None]
        link_imag = link_field[1, :, b][..., None]
        term_real = link_real * vectors[0, b] - link_imag * vectors[1, b]
        term_imag = link_real * vectors[1, b] + link_imag * vectors[0, b]
        if b == 0:
            total_real, total_imag = (term_real, term_imag)
        else:
            total_real, total_imag = (total_real + term_real, total_imag + term_imag)
    return jnp.stack([total_real, total_imag])


def apply_adjoint(link_field, vectors):
    for b in range(3):
        link_real = link_field[0, b][..., None]
        link_imag = link_field[1, b][..., None]
        term_real = link_real * vectors[0, b] + link_imag * vectors[1, b]
        term_imag = link_real * vectors[1, b] - link_imag * vectors[0, b]
        if b == 0:
            total_real, total_imag = (term_real, term_imag)
        else:
            total_real, total_imag = (total_real + term_real, total_imag + term_imag)
    return jnp.stack([total_real, total_imag])


def phase_field(vectors, z_coord, z_total):
    angles = 2.0 * math.pi / z_total * z_coord
    cosine_part = jnp.cos(angles)[:, None, None, None]
    sine_part = jnp.sin(angles)[:, None, None, None]
    return jnp.stack(
        [
            cosine_part * vectors[0] + sine_part * vectors[1],
            cosine_part * vectors[1] - sine_part * vectors[0],
        ]
    )


def covariant(direction, vectors, link_field, upper_rim, lower_rim):
    roll_axis = 4 - direction
    links_along = link_field[direction]
    forward = apply_links(links_along, jnp.roll(vectors, -1, roll_axis))
    backward = jnp.roll(apply_adjoint(links_along, vectors), 1, roll_axis)
    return 0.5 * (forward - backward)


def covariant_third(vectors, link_field, upper_rim, lower_rim):
    links_along = link_field[2]
    forward = apply_links(links_along, jnp.concatenate([vectors[:, :, 1:], upper_rim], axis=2))
    inner = apply_adjoint(links_along[:, :, :, :-1], vectors[:, :, :-1])
    backward = jnp.concatenate([lower_rim, inner], axis=2)
    return 0.5 * (forward - backward)


def gram_block(vectors_half, displaced, scaling):
    columns = vectors_half.shape[-1]
    left_side = vectors_half.reshape(-1, columns)
    displaced_half = displaced.astype(jnp.bfloat16)
    field_real = displaced_half[0].reshape(-1, columns)
    field_imag = displaced_half[1].reshape(-1, columns)
    right_side = jnp.concatenate(
        [
            jnp.concatenate([field_real, field_imag], 0),
            jnp.concatenate([field_imag, -field_real], 0),
        ],
        1,
    )
    product = lax.dot_general(
        left_side, right_side, (((0,), (0,)), ((), ())), preferred_element_type=jnp.float32
    )
    return (product * scaling).reshape(columns, 2, columns)


def contract_pair(source, sink_matrix, blocks, pair_signs):
    columns = source.shape[-1]
    sink_block = jnp.concatenate(
        [
            jnp.concatenate([sink_matrix[:, 0], -sink_matrix[:, 1]], 1),
            jnp.concatenate([sink_matrix[:, 1], sink_matrix[:, 0]], 1),
        ],
        0,
    )
    source_block = jnp.concatenate(
        [
            jnp.concatenate([source[:, 0], source[:, 1]], 1),
            jnp.concatenate([-source[:, 1], source[:, 0]], 1),
        ],
        0,
    )
    source_block = source_block.reshape(2, columns, 2 * columns)
    stacked = blocks.reshape(blocks.shape[0], 2 * columns, columns)
    halfway = jnp.einsum(
        "mk,qkn->qmn", sink_block, stacked, preferred_element_type=jnp.float32
    ).astype(jnp.bfloat16)
    second = jnp.einsum(
        "qcmk,ckn->qmn",
        halfway.reshape(-1, 2, columns, columns),
        source_block,
        preferred_element_type=jnp.float32,
    )
    tau_real = blocks[:, 0].astype(jnp.float32)
    tau_imag = blocks[:, 1].astype(jnp.float32)
    out_real = second[:, :, :columns]
    out_imag = second[:, :, columns:]
    trace_real = jnp.sum(out_real * tau_real + out_imag * tau_imag, axis=(1, 2))
    trace_imag = jnp.sum(out_imag * tau_real - out_real * tau_imag, axis=(1, 2))
    return jnp.stack([jnp.sum(pair_signs * trace_real), jnp.sum(pair_signs * trace_imag)]) / (
        4.0 * columns
    )


def shards(eigvecs, links, directions, pair_list, pair_operators, perambulators):
    slices = eigvecs.shape[0]
    local_sites = eigvecs.shape[3]
    columns = eigvecs.shape[4]
    plane_sites = PX * PY
    plane_count = local_sites // plane_sites
    layers = lax.axis_size("space")
    z_total = plane_count * layers
    scaling = 1.0 / math.sqrt(6.0 * plane_sites * z_total)
    z_coord = (lax.axis_index("space") * plane_count + jnp.arange(plane_count)).astype(jnp.float32)
    plane_above = from_behind(eigvecs[:, :, :, :plane_sites], "space", -1)
    top_vectors = eigvecs[:, :, :, local_sites - plane_sites :]
    top_links = links[:, 2, :, :, :, local_sites - plane_sites :]
    moved_vectors = from_behind(top_vectors, "space", 1)
    moved_links = from_behind(top_links, "space", 1)
    plane_below = jax.vmap(apply_adjoint)(
        moved_links.astype(jnp.float32), moved_vectors.astype(jnp.float32)
    )
    branches = [
        partial(covariant, 0),
        partial(covariant, 1),
        covariant_third,
        lambda vectors, link_field, upper_rim, lower_rim: phase_field(vectors, z_coord, z_total),
    ]
    op_slots = directions.shape[0]

    def per_slice(inputs):
        vectors_half, link_half, above_half, below_slice = inputs
        vectors = vectors_half.astype(jnp.float32).reshape(2, 3, plane_count, PY, PX, columns)
        link_field = link_half.astype(jnp.float32).reshape(3, 2, 3, 3, plane_count, PY, PX)
        upper_rim = above_half.astype(jnp.float32).reshape(2, 3, 1, PY, PX, columns)
        lower_rim = below_slice.reshape(2, 3, 1, PY, PX, columns)
        blocks = []
        for op_slot in range(op_slots):
            displaced = lax.switch(
                directions[op_slot], branches, vectors, link_field, upper_rim, lower_rim
            )
            blocks.append(gram_block(vectors_half, displaced, scaling))
        return jnp.stack(blocks)

    partials = lax.map(per_slice, (eigvecs, links, plane_above, plane_below))
    spin_size = lax.axis_size("spin")
    totals = lax.psum(partials, "space")
    row_count = columns // layers
    elementals = lax.dynamic_slice_in_dim(totals, lax.axis_index("space") * row_count, row_count, 2)
    elemental_table = lax.all_gather(
        totals.astype(jnp.bfloat16)[None], ("tm", "spin"), axis=0, tiled=True
    )
    flattened = elemental_table.reshape(-1, columns, 2, columns)
    position = (
        (pair_list // slices * spin_size + pair_operators // op_slots) * slices + pair_list % slices
    ) * op_slots + pair_operators % op_slots
    source_rows = flattened[position[:, 0]]
    sink_rows = flattened[position[:, 1]]
    pair_count = perambulators.shape[1]
    spin_pair = lax.axis_index("spin") * pair_count + jnp.arange(pair_count)
    first_sign = jnp.where(spin_pair // 4 < 2, 1.0, -1.0)
    later_sign = jnp.where(spin_pair % 4 < 2, 1.0, -1.0)
    pair_signs = (first_sign * later_sign).astype(jnp.float32)

    def per_pair(inputs):
        source, sink_matrix, blocks = inputs
        return contract_pair(source, sink_matrix, blocks, pair_signs)

    partial_corr = lax.map(per_pair, (source_rows, sink_rows, perambulators))
    correlators = lax.psum(partial_corr, "spin")
    return (elementals, correlators)


def solution(mesh):
    return jax.shard_map(
        shards,
        mesh=mesh,
        in_specs=(
            P("tm", None, None, "space", None),
            P("tm", None, None, None, None, "space"),
            P("spin"),
            P(("space", "tm"), None),
            P(("space", "tm"), None),
            P(("space", "tm"), "spin", None, None, None),
        ),
        out_specs=(P(("ens", "tm"), "spin", "space", None, None), P(("ens", "space", "tm"), None)),
        check_vma=False,
    )
```

profile of v0, /device:TPU:0, one launch (start us, length us, event | category | flops | bytes accessed | tf_op | source)
XLA Modules:
  0.0 290.5 jit_solution(11844642984709961674)
XLA Ops:
  8.0 3.1 %collective-permute-start.1 = (bf16[2,2,3,3,256]{4,1,3,2,0:T(2,128)(2,1)S(1)}, bf16[2,2,3,3,256]{4,1,3,2,0:T(2,128)(2,1)S(1)}, u32[]{:S(2)}, u32[]{:S(2)}) collective-permute-start(bf16[2,2,3,3,256]{4,1,3,2,0:T(2,128)(2,1)S(1)} %slice_bitcast_fusion.126), channel_id=1, source_target_pairs={{0,4},{4,8},{8,12},{12,0},{1,5},{5,9},{9,13},{13,1},{2,6},{6,10},{... | collective-permute-start | bytes 55304 | tf_op jit(solution)/shard_map/ppermute | solution.py:15
  11.1 2.4 fusion.140
  13.5 1.6 collective-permute-start.2
  15.1 2.2 collective-permute-start
  19.4 16.4 %collective-permute-done.2 = bf16[2,2,3,256,128]{4,3,2,1,0:T(8,128)(2,1)S(1)} collective-permute-done((bf16[2,2,3,256,128]{4,3,2,1,0:T(8,128)(2,1)S(1)}, bf16[2,2,3,256,128]{4,3,2,1,0:T(8,128)(2,1)S(1)}, u32[]{:S(2)}, u32[]{:S(2)}) %collective-permute-start.2) | collective-permute-done | bytes 786464 | tf_op jit(solution)/shard_map/ppermute | solution.py:15
  36.0 1.4 add_add_fusion.12
  37.4 1.2 maximum_bitcast_fusion.3
  38.7 12.3 %collective-permute-done = bf16[2,2,3,256,128]{4,3,2,1,0:T(8,128)(2,1)} collective-permute-done((bf16[2,2,3,256,128]{4,3,2,1,0:T(8,128)(2,1)}, bf16[2,2,3,256,128]{4,3,2,1,0:T(8,128)(2,1)}, u32[]{:S(2)}, u32[]{:S(2)}) %collective-permute-start) | collective-permute-done | bytes 786464 | tf_op jit(solution)/shard_map/ppermute | solution.py:15
  51.0 112.4 %while.24 = (s32[]{:T(128)}, f32[2,2,128,2,128]{4,2,3,1,0:T(8,128)}, bf16[2,2,3,2048,128]{4,3,2,1,0:T(8,128)(2,1)}, bf16[2,3,2,3,3,2048]{5,2,4,3,1,0:T(2,128)(2,...) while((s32[]{:T(128)}, ...), condition=%wide.region_9.10_spmd.clone, body=%wide.region_0.9_spmd.clone.sunk | while | flops 1758900224 | bytes 315630656 | solution.py:169
  51.0 2.1 constant_dynamic-slice_fusion.11
  53.1 3.7 %convert.50 = f32[2,3,8,16,16,128]{5,4,3,2,1,0:T(8,128)} convert(bf16[2,3,8,16,16,128]{5,4,3,2,1,0:T(8,128)(2,1)S(1)} %bitcast.469) | non-fusion elementwise | flops 1572864 | bytes 9437184 | tf_op jit(solution)/shard_map/while/body/eval_jaxpr/convert_element_type | solution.py:157
  56.8 1.1 dynamic-slice_convert_fusion.2
  57.9 2.3 reshape.1168
  60.2 1.0 constant_dynamic-slice_fusion.12
  61.3 1.5 constant_dynamic-slice_fusion.13
  63.7 22.8 %conditional.7 = (bf16[6144,128]{1,0:T(8,128)(2,1)S(1)}, bf16[6144,128]{1,0:T(8,128)(2,1)S(1)}) conditional(s32[]{:T(128)} %get-tuple-element.872, (f32[3,2,3,3,8,16,16]{6,5,4,1,3,2,0:T(8,128)S(1)}, f32[2,3,8,16,16,128]{5,4,3,2,1,0:T(8,128)}) %tuple.370, (f32[3,2,3,3,8,16,16]{6,5,4,1,3,2,0:T(8,128)S(1)}, ...), branch_computations={%region_1.1_spmd, %region_2.2_spmd, %region_3.3_spmd, %region_4.4_... | conditional | flops 47185920 | bytes 112312368 | solution.py:163
  69.9 3.0 %slice_bitcast_fusion.44 = (f32[7,16,16,128]{3,2,1,0:T(8,128)S(1)}, f32[7,16,16,128]{3,2,1,0:T(8,128)S(1)}, f32[7,16,16,128]{3,2,1,0:T(8,128)S(1)}, f32[7,16,16,...) fusion(f32[2,3,8,16,16,128]{5,4,3,2,1,0:T(8,128)} %get-tuple-element.315), kind=kLoop, calls=%fused_computation.141 | loop fusion | bytes 11010048 | tf_op jit(solution)/shard_map/while/body/eval_jaxpr/cond/branch_2_fun/mul | solution.py:35
  73.1 4.5 %add_add_fusion.5 = (f32[1,3,7,16,16,128]{5,4,3,2,1,0:T(8,128)S(1)}, f32[1,3,7,16,16,128]{5,4,3,2,1,0:T(8,128)S(1)}) fusion(f32[7,16,16,128]{3,2,1,0:T(8,128)S(1)} %get-tuple-element.561, f32[3,7,16,16]{3,2,1,0:T(8,128)S(1)} %get-tuple-element.571, f32[7,16,16,128]{3,2,1,0:T(8,128)S(1)} %get-tuple-element.557, f32[3,7,16,16]{3,2,1,0:T(8,128)S(1)} %get-tuple-element.572, ...), kind=kLoop, calls=%fused_computation.122 | loop fusion | flops 15138816 | bytes 11139072 | tf_op jit(solution)/shard_map/while/body/eval_jaxpr/cond/branch_2_fun/add | solution.py:40
  79.0 5.2 %subtract_add_fusion.4 = (f32[1,3,8,16,16,128]{5,4,3,2,1,0:T(8,128)S(1)}, f32[1,3,8,16,16,128]{5,4,3,2,1,0:T(8,128)S(1)}) fusion(f32[8,16,16,128]{3,2,1,0:T(8,128)S(1)} %get-tuple-element.566, f32[3,8,16,16]{3,2,1,0:T(8,128)S(1)} %get-tuple-element.577, f32[8,16,16,128]{3,2,1,0:T(8,128)S(1)} %get-tuple-element.567, ...), kind=kLoop, calls=%fused_computation.120 | loop fusion | flops 17301504 | bytes 12730368 | tf_op jit(solution)/shard_map/while/body/eval_jaxpr/cond/branch_2_fun/add | solution.py:27
  84.2 1.3 fusion.35
  86.8 1.6 copy-done.5
  88.4 1.8 fusion.172
  90.2 1.6 reshape.1170
  91.8 9.9 %conditional.6 = (bf16[6144,128]{1,0:T(8,128)(2,1)S(1)}, bf16[6144,128]{1,0:T(8,128)(2,1)S(1)}) conditional(s32[]{:T(128)} %get-tuple-element.873, (f32[3,2,3,3,8,16,16]{6,5,4,1,3,2,0:T(8,128)S(1)}, f32[2,3,8,16,16,128]{5,4,3,2,1,0:T(8,128)}) %tuple.370, (f32[3,2,3,3,8,16,16]{6,5,4,1,3,2,0:T(8,128)S(1)}, ...), branch_computations={%region_5.5_spmd, %region_6.6_spmd, %region_7.7_spmd, %region_8.8_... | conditional | flops 47185920 | bytes 112312368 | solution.py:163
  98.0 3.8 %subtract_convert_fusion.1 = (bf16[1,3,8,16,16,128]{5,4,3,2,1,0:T(8,128)(2,1)S(1)}, bf16[1,3,8,16,16,128]{5,4,3,2,1,0:T(8,128)(2,1)S(1)}) fusion(f32[2,3,8,16,16,128]{5,4,3,2,1,0:T(8,128)} %get-tuple-element.329, f32[8]{0:T(128)S(1)} %get-tuple-element.679, f32[8]{0:T(128)S(1)} %get-tuple-element.678), kind=kLoop, calls=%fused_computation.308 | loop fusion | flops 6291456 | bytes 9437248 | tf_op jit(solution)/shard_map/convert.5
  102.1 1.6 copy-done.6
  103.7 1.2 fusion.171
  106.2 2.1 constant_dynamic-slice_fusion.11
  108.4 3.7 %convert.50 = f32[2,3,8,16,16,128]{5,4,3,2,1,0:T(8,128)} convert(bf16[2,3,8,16,16,128]{5,4,3,2,1,0:T(8,128)(2,1)S(1)} %bitcast.469) | non-fusion elementwise | flops 1572864 | bytes 9437184 | tf_op jit(solution)/shard_map/while/body/eval_jaxpr/convert_element_type | solution.py:157
  112.1 1.1 dynamic-slice_convert_fusion.2
  113.1 2.3 reshape.1168
  115.4 1.0 constant_dynamic-slice_fusion.12
  116.6 1.5 constant_dynamic-slice_fusion.13
  118.9 22.6 %conditional.7 = (bf16[6144,128]{1,0:T(8,128)(2,1)S(1)}, bf16[6144,128]{1,0:T(8,128)(2,1)S(1)}) conditional(s32[]{:T(128)} %get-tuple-element.872, (f32[3,2,3,3,8,16,16]{6,5,4,1,3,2,0:T(8,128)S(1)}, f32[2,3,8,16,16,128]{5,4,3,2,1,0:T(8,128)}) %tuple.370, (f32[3,2,3,3,8,16,16]{6,5,4,1,3,2,0:T(8,128)S(1)}, ...), branch_computations={%region_1.1_spmd, %region_2.2_spmd, %region_3.3_spmd, %region_4.4_... | conditional | flops 47185920 | bytes 112312368 | solution.py:163
  125.0 3.0 %slice_bitcast_fusion.44 = (f32[7,16,16,128]{3,2,1,0:T(8,128)S(1)}, f32[7,16,16,128]{3,2,1,0:T(8,128)S(1)}, f32[7,16,16,128]{3,2,1,0:T(8,128)S(1)}, f32[7,16,16,...) fusion(f32[2,3,8,16,16,128]{5,4,3,2,1,0:T(8,128)} %get-tuple-element.315), kind=kLoop, calls=%fused_computation.141 | loop fusion | bytes 11010048 | tf_op jit(solution)/shard_map/while/body/eval_jaxpr/cond/branch_2_fun/mul | solution.py:35
  128.2 4.5 %add_add_fusion.5 = (f32[1,3,7,16,16,128]{5,4,3,2,1,0:T(8,128)S(1)}, f32[1,3,7,16,16,128]{5,4,3,2,1,0:T(8,128)S(1)}) fusion(f32[7,16,16,128]{3,2,1,0:T(8,128)S(1)} %get-tuple-element.561, f32[3,7,16,16]{3,2,1,0:T(8,128)S(1)} %get-tuple-element.571, f32[7,16,16,128]{3,2,1,0:T(8,128)S(1)} %get-tuple-element.557, f32[3,7,16,16]{3,2,1,0:T(8,128)S(1)} %get-tuple-element.572, ...), kind=kLoop, calls=%fused_computation.122 | loop fusion | flops 15138816 | bytes 11139072 | tf_op jit(solution)/shard_map/while/body/eval_jaxpr/cond/branch_2_fun/add | solution.py:40
  134.1 5.2 %subtract_add_fusion.4 = (f32[1,3,8,16,16,128]{5,4,3,2,1,0:T(8,128)S(1)}, f32[1,3,8,16,16,128]{5,4,3,2,1,0:T(8,128)S(1)}) fusion(f32[8,16,16,128]{3,2,1,0:T(8,128)S(1)} %get-tuple-element.566, f32[3,8,16,16]{3,2,1,0:T(8,128)S(1)} %get-tuple-element.577, f32[8,16,16,128]{3,2,1,0:T(8,128)S(1)} %get-tuple-element.567, ...), kind=kLoop, calls=%fused_computation.120 | loop fusion | flops 17301504 | bytes 12730368 | tf_op jit(solution)/shard_map/while/body/eval_jaxpr/cond/branch_2_fun/add | solution.py:27
  139.3 1.3 fusion.35
  141.9 1.6 copy-done.5
  143.5 1.8 fusion.172
  145.3 1.6 reshape.1170
  146.9 10.3 %conditional.6 = (bf16[6144,128]{1,0:T(8,128)(2,1)S(1)}, bf16[6144,128]{1,0:T(8,128)(2,1)S(1)}) conditional(s32[]{:T(128)} %get-tuple-element.873, (f32[3,2,3,3,8,16,16]{6,5,4,1,3,2,0:T(8,128)S(1)}, f32[2,3,8,16,16,128]{5,4,3,2,1,0:T(8,128)}) %tuple.370, (f32[3,2,3,3,8,16,16]{6,5,4,1,3,2,0:T(8,128)S(1)}, ...), branch_computations={%region_5.5_spmd, %region_6.6_spmd, %region_7.7_spmd, %region_8.8_... | conditional | flops 47185920 | bytes 112312368 | solution.py:163
  153.4 3.8 %subtract_convert_fusion.1 = (bf16[1,3,8,16,16,128]{5,4,3,2,1,0:T(8,128)(2,1)S(1)}, bf16[1,3,8,16,16,128]{5,4,3,2,1,0:T(8,128)(2,1)S(1)}) fusion(f32[2,3,8,16,16,128]{5,4,3,2,1,0:T(8,128)} %get-tuple-element.329, f32[8]{0:T(128)S(1)} %get-tuple-element.679, f32[8]{0:T(128)S(1)} %get-tuple-element.678), kind=kLoop, calls=%fused_computation.308 | loop fusion | flops 6291456 | bytes 9437248 | tf_op jit(solution)/shard_map/convert.5
  157.5 1.6 copy-done.6
  159.1 1.2 fusion.171
  163.5 69.8 %all-reduce.2.cloned.1.call-done = f32[2,2,128,2,128]{4,2,3,1,0:T(8,128)} async-done(((f32[2,2,128,2,128]{4,2,3,1,0:T(8,128)}), f32[2,2,128,2,128]{4,2,3,1,0:T(8,128)}) %all-reduce.2.cloned.1.call-update) | async-done | bytes 524304 | tf_op jit(solution)/shard_map/psum | solution.py:171
  233.3 1.8 convert_element_type.114
  236.9 14.9 %all-gather.3.cloned.1.call-done = bf16[8,2,128,2,128]{4,2,3,1,0:T(8,128)(2,1)} async-done(((bf16[2,2,128,2,128]{4,2,3,1,0:T(8,128)(2,1)}), bf16[8,2,128,2,128]{4,2,3,1,0:T(8,128)(2,1)}) %all-gather.3.cloned.1.call-update) | async-done | bytes 1048592 | tf_op jit(solution)/shard_map/all_gather | solution.py:174
  251.8 1.8 gather_fusion
  253.6 1.8 gather_fusion.1
  255.4 25.0 %while.25 = (s32[]{:T(128)}, f32[4,2]{0,1:T(2,128)S(1)}, bf16[4,8,2,128,128]{4,3,2,1,0:T(8,128)(2,1)}, bf16[4,128,2,128]{3,1,2,0:T(8,128)(2,1)S(1)}, bf16[4,128,...) while((s32[]{:T(128)}, f32[4,2]{0,1:T(2,128)S(1)}, ...), condition=%wide.region_16.17_spmd.clone, body=%wide.region_11.16_spmd.clone.sunk | while | flops 271090112 | bytes 8454929 | solution.py:193
  255.5 1.1 constant_dynamic-slice_fusion.15
  257.6 1.1 copy_bitcast_fusion.8
  260.3 1.3 maximum_multiply_fusion.2
  261.7 1.1 constant_dynamic-slice_fusion.15
  263.8 1.1 copy_bitcast_fusion.8
  266.5 1.3 maximum_multiply_fusion.2
  268.0 1.1 constant_dynamic-slice_fusion.15
  270.1 1.1 copy_bitcast_fusion.8
  272.8 1.3 maximum_multiply_fusion.2
  274.2 1.1 constant_dynamic-slice_fusion.15
  276.3 1.1 copy_bitcast_fusion.8
  279.0 1.3 maximum_multiply_fusion.2
  280.4 3.0 %psum.15 = f32[4,2]{0,1:T(2,128)} all-reduce(f32[4,2]{0,1:T(2,128)S(1)} %get-tuple-element.356), channel_id=1, replica_groups=mesh['ens'=2,'space'=4,'tm'=2,'spin'=2] {'spin'}, use_global_device_ids=true, to_apply=%region_17.18 | all-reduce | flops 8 | bytes 64 | tf_op jit(solution)/shard_map/psum | solution.py:194
  (146 shorter events, 24.4 us)
Async XLA Ops:
  7.2 10.2 %copy-start.13 = (s32[2]{0:T(128)S(1)}, s32[2]{0:T(128)}, u32[]{:S(2)}) copy-start(s32[2]{0:T(128)} %param.20) | copy-start | bytes 28
  7.2 226.1 %all-reduce.2.cloned.1.call-start = ((), (), s32[]{:S(2)}) async-start(), calls=%async_computation | async-start | bytes 1048576 | tf_op jit(solution)/shard_map/psum | solution.py:171
  8.0 11.3 %collective-permute-start.1 = (bf16[2,2,3,3,256]{4,1,3,2,0:T(2,128)(2,1)S(1)}, bf16[2,2,3,3,256]{4,1,3,2,0:T(2,128)(2,1)S(1)}, u32[]{:S(2)}, u32[]{:S(2)}) collective-permute-start(bf16[2,2,3,3,256]{4,1,3,2,0:T(2,128)(2,1)S(1)} %slice_bitcast_fusion.126), channel_id=1, source_target_pairs={{0,4},{4,8},{8,12},{12,0},{1,5},{5,9},{9,13},{13,1},{2,6},{6,10},{... | collective-permute-start | bytes 55304 | tf_op jit(solution)/shard_map/ppermute | solution.py:15
  13.5 22.3 %collective-permute-start.2 = (bf16[2,2,3,256,128]{4,3,2,1,0:T(8,128)(2,1)S(1)}, bf16[2,2,3,256,128]{4,3,2,1,0:T(8,128)(2,1)S(1)}, u32[]{:S(2)}, u32[]{:S(2)}) collective-permute-start(bf16[2,2,3,256,128]{4,3,2,1,0:T(8,128)(2,1)S(1)} %get-tuple-element.686), channel_id=1, source_target_pairs={{0,4},{4,8},{8,12},{12,0},{1,5},{5,9},{9,13},{13,1},{2,6},{6,10},{... | collective-permute-start | bytes 2359304 | tf_op jit(solution)/shard_map/ppermute | solution.py:15
  15.1 35.9 %collective-permute-start = (bf16[2,2,3,256,128]{4,3,2,1,0:T(8,128)(2,1)}, bf16[2,2,3,256,128]{4,3,2,1,0:T(8,128)(2,1)}, u32[]{:S(2)}, u32[]{:S(2)}) collective-permute-start(bf16[2,2,3,256,128]{4,3,2,1,0:T(8,128)(2,1)} %get-tuple-element.687), channel_id=1, source_target_pairs={{0,12},{4,0},{8,4},{12,8},{1,13},{5,1},{9,5},{13,9},{2,14},{6,2},{... | collective-permute-start | bytes 2359304 | tf_op jit(solution)/shard_map/ppermute | solution.py:15
  51.0 184.2 %copy-start.14 = (s32[4,2]{0,1:T(2,128)S(1)}, s32[4,2]{0,1:T(2,128)}, u32[]{:S(2)}) copy-start(s32[4,2]{0,1:T(2,128)} %param.22) | copy-start | bytes 100
  51.0 184.2 %copy-start.15 = (s32[4,2]{0,1:T(2,128)S(1)}, s32[4,2]{0,1:T(2,128)}, u32[]{:S(2)}) copy-start(s32[4,2]{0,1:T(2,128)} %param.21) | copy-start | bytes 100
  53.1 3.7 %copy-start.4 = (bf16[1,2,3,2048,128]{4,3,2,1,0:T(8,128)(2,1)}, bf16[1,2,3,2048,128]{4,3,2,1,0:T(8,128)(2,1)S(1)}, u32[]{:S(2)}) copy-start(bf16[1,2,3,2048,128]{4,3,2,1,0:T(8,128)(2,1)S(1)} %constant_dynamic-slice_fusion.11) | copy-start | bytes 9437188 | tf_op jit(solution)/shard_map/while
  53.1 3.7 %copy-start.12 = (bf16[2,3,2,3,3,2048]{5,2,4,3,1,0:T(2,128)(2,1)S(1)}, bf16[2,3,2,3,3,2048]{5,2,4,3,1,0:T(2,128)(2,1)}, u32[]{:S(2)}) copy-start(bf16[2,3,2,3,3,2048]{5,2,4,3,1,0:T(2,128)(2,1)} %get-tuple-element.869) | copy-start | bytes 1327108 | tf_op jit(solution)/shard_map/while
  61.3 1.5 copy-start.7
  62.8 0.9 copy-start.9
  73.1 4.5 %slice-start = ((s8[6291456]{0:T(1024)(128)(4,1)}), s8[4194304]{0:T(1024)(128)(4,1)S(1)}, s32[]{:S(2)}) async-start(s8[6291456]{0:T(1024)(128)(4,1)} %bitcast.465), calls=%async_computation.2 | async-start | bytes 8388608 | tf_op jit(solution)/shard_map/while/body/eval_jaxpr/cond
  73.1 4.5 %slice-start.1 = ((s8[6291456]{0:T(1024)(128)(4,1)}), s8[2097152]{0:T(1024)(128)(4,1)S(1)}, s32[]{:S(2)}) async-start(s8[6291456]{0:T(1024)(128)(4,1)} %bitcast.465), calls=%async_computation.3 | async-start | bytes 4194304 | tf_op jit(solution)/shard_map/while/body/eval_jaxpr/cond
  86.5 1.9 copy-start.5
  101.8 1.9 copy-start.6
  103.7 1.3 copy-start.11
  108.3 3.7 %copy-start.4 = (bf16[1,2,3,2048,128]{4,3,2,1,0:T(8,128)(2,1)}, bf16[1,2,3,2048,128]{4,3,2,1,0:T(8,128)(2,1)S(1)}, u32[]{:S(2)}) copy-start(bf16[1,2,3,2048,128]{4,3,2,1,0:T(8,128)(2,1)S(1)} %constant_dynamic-slice_fusion.11) | copy-start | bytes 9437188 | tf_op jit(solution)/shard_map/while
  108.4 3.7 %copy-start.12 = (bf16[2,3,2,3,3,2048]{5,2,4,3,1,0:T(2,128)(2,1)S(1)}, bf16[2,3,2,3,3,2048]{5,2,4,3,1,0:T(2,128)(2,1)}, u32[]{:S(2)}) copy-start(bf16[2,3,2,3,3,2048]{5,2,4,3,1,0:T(2,128)(2,1)} %get-tuple-element.869) | copy-start | bytes 1327108 | tf_op jit(solution)/shard_map/while
  116.6 1.5 copy-start.7
  118.0 0.9 copy-start.9
  128.2 4.5 %slice-start = ((s8[6291456]{0:T(1024)(128)(4,1)}), s8[4194304]{0:T(1024)(128)(4,1)S(1)}, s32[]{:S(2)}) async-start(s8[6291456]{0:T(1024)(128)(4,1)} %bitcast.465), calls=%async_computation.2 | async-start | bytes 8388608 | tf_op jit(solution)/shard_map/while/body/eval_jaxpr/cond
  128.2 4.5 %slice-start.1 = ((s8[6291456]{0:T(1024)(128)(4,1)}), s8[2097152]{0:T(1024)(128)(4,1)S(1)}, s32[]{:S(2)}) async-start(s8[6291456]{0:T(1024)(128)(4,1)} %bitcast.465), calls=%async_computation.3 | async-start | bytes 4194304 | tf_op jit(solution)/shard_map/while/body/eval_jaxpr/cond
  141.6 1.9 copy-start.5
  157.2 1.9 copy-start.6
  159.1 1.3 copy-start.11
  163.5 88.3 %all-gather.3.cloned.1.call-start = ((), (), s32[]{:S(2)}) async-start(), calls=%async_computation.1 | async-start | bytes 1310720 | tf_op jit(solution)/shard_map/all_gather | solution.py:174
Sparse Core Ops, SparseCore 0:
  163.6 69.6 all-reduce.1
  235.2 16.4 all-gather.2
where the time goes:
time: 296 us; the launch traced here: 291 us
  waiting for transfers between devices  113 us (38%)
  other arithmetic  58.5 us (20%)
  local copies, waits for them, and re-layouts  55.9 us (19%)
  loops' own time  28.3 us (10%)
  between operations  15.8 us (5%)
  matrix products  8.55 us (3%)
  starting transfers between devices  7.01 us (2%)
  blocking collectives  3.01 us (1%)
    psum x1, waiting for transfers between devices, shards(): totals = lax.psum(partials, 'space')  69.8 us
    ppermute x3, waiting for transfers between devices, from_behind(): lax.ppermute(array, axis, [(i, (i + by) % count) for i in range(count)])  28.7 us
    another operation x4, loops' own time, per_slice(): lax.switch(directions[op_slot], branches, vectors, link_field, upper_rim,...  24.9 us
    all_gather x1, waiting for transfers between devices, shards(): lax.all_gather(totals.astype(jnp.bfloat16)[None], ('tm', 'spin'), axis=0,...  14.9 us
    add x2, other arithmetic, apply_links(): total_real, total_imag = (total_real + term_real, total_imag + term_imag)  10.5 us
    add x3, other arithmetic, apply_adjoint(): total_real, total_imag = (total_real + term_real, total_imag + term_imag)  10.3 us
    dynamic_slice x6, local copies, waits for them, and re-layouts, shards(): partials = lax.map(per_slice, (eigvecs, links, plane_above, plane_below))  9.22 us
    while x28, local copies, waits for them, and re-layouts  8.02 us
  transfers between devices with their start and end apart: 5, of which 4 were waited for; matrix products, arithmetic and copies ran while one was open for 3% of the time, Pallas kernels for 0%

commit v1 on v0

v1 whole, which is shorter than its diff:
```python
from functools import partial
import math

import jax
import jax.numpy as jnp
from jax import lax
from jax.experimental import pallas as pl
from jax.experimental.pallas import tpu as pltpu
from jax.sharding import PartitionSpec as P

PX = 16
PY = 16
LANES = 128
ROWS = 8


def flip(array, axis, mask):
    count = lax.axis_size(axis)
    return lax.ppermute(array, axis, [(i, i ^ mask) for i in range(count)])


def flip_both(array, space_mask, tm_mask):
    space, tm = lax.axis_size("space"), lax.axis_size("tm")
    pairs = [
        (z * tm + x, (z ^ space_mask) * tm + (x ^ tm_mask)) for z in range(space) for x in range(tm)
    ]
    return lax.ppermute(array, ("space", "tm"), pairs)


def transposed_plane(v_ref, vt_ref):
    for part in range(2):
        for colour in range(3):
            vt_ref[3 * part + colour] = v_ref[part, colour].astype(jnp.float32).T


def stacked_plane(v_ref, vr_ref, shift=0):
    sites = v_ref.shape[2]
    for part in range(2):
        columns = slice(part * LANES, (part + 1) * LANES)
        for colour in range(3):
            start = colour * sites
            if shift:
                vr_ref[start : start + shift, columns] = v_ref[part, colour, sites - shift :]
            vr_ref[start + shift : start + sites, columns] = v_ref[part, colour, : sites - shift]


def permuted_plane(v_ref, vr_ref, permutation):
    sites = v_ref.shape[2]
    for colour in range(3):
        plane = jnp.concatenate([v_ref[0, colour], v_ref[1, colour]], 1)
        vr_ref[colour * sites : (colour + 1) * sites] = dot(permutation, plane).astype(jnp.bfloat16)


def link_sums(u, uf_ref):
    real, imag = u[..., 0:1, :], u[..., 1:2, :]
    uf_ref[..., 0:1, :] = real
    uf_ref[..., 1:2, :] = imag - real
    uf_ref[..., 2:3, :] = imag + real


def turned(u, amount):
    sites = u.shape[-1]
    return jnp.concatenate([u[..., sites - amount :], u[..., : sites - amount]], -1)


def link_rows(uf_ref, lead, lanes):
    return [
        [[uf_ref[lead + (a, b, slice(i, i + 1), lanes)] for b in range(3)] for a in range(3)]
        for i in range(3)
    ]


def times_links(rows, vectors, f_ref, k_tile, lanes, sites):
    sums = [vectors[0][b] + vectors[1][b] for b in range(3)]
    for a in range(3):
        k1 = sum_products(rows[0][a], sums)
        k2 = sum_products(rows[1][a], vectors[0])
        k3 = sum_products(rows[2][a], vectors[1])
        for part, value in ((0, k1 - k3), (1, k1 + k2)):
            start = part * LANES + k_tile * ROWS
            high = value.astype(jnp.bfloat16)
            low = (value - high.astype(jnp.float32)).astype(jnp.bfloat16)
            columns = slice(a * sites + lanes.start, a * sites + lanes.stop)
            for copy, piece in ((0, high), (1, low)):
                at = copy * 2 * LANES + start
                f_ref[at : at + ROWS, columns] = piece


def direction(rows_of, vt, f_ref):
    sites = vt.shape[2]
    for j in range(sites // LANES):
        lanes = slice(j * LANES, (j + 1) * LANES)
        rows = rows_of(lanes)
        for k_tile in range(LANES // ROWS):
            k = slice(k_tile * ROWS, (k_tile + 1) * ROWS)
            vectors = [[vt[3 * part + c, k, lanes] for c in range(3)] for part in range(2)]
            times_links(rows, vectors, f_ref, k_tile, lanes, sites)


def gram(f_ref, vr_ref):
    both = dot(f_ref[...], vr_ref[...])
    return both[: 2 * LANES] + both[2 * LANES :]


def sum_products(left, right):
    return left[0] * right[0] + left[1] * right[1] + left[2] * right[2]


def block(acc, q, p):
    return acc[q * LANES : (q + 1) * LANES, p * LANES : (p + 1) * LANES]


def upper(shape):
    row = lax.broadcasted_iota(jnp.int32, shape, 0)
    column = lax.broadcasted_iota(jnp.int32, shape, 1)
    return row <= column


def antihermitian(acc, scale):
    real = block(acc, 0, 0) + block(acc, 1, 1)
    imag = block(acc, 1, 0) - block(acc, 0, 1)
    e_real = scale * (real.T - real)
    e_imag = scale * (imag.T + imag)
    return jnp.where(upper(real.shape), e_imag, e_real)


def dot(left, right):
    return jnp.dot(left, right, preferred_element_type=jnp.float32)


def store_halves(out_ref, at, matrix, parity):
    half_rows = matrix.shape[0] // 2
    for half in range(2):
        out_ref[parity ^ half, at] = matrix[half * half_rows : (half + 1) * half_rows]


def plane_kernel(
    where_ref, v_ref, u_ref, below_ref, out_ref, inner_ref, waves, vt, vtb, vr, vx, vy, vz, uf, f0, f1, f2, acc, *, scale, step
):
    plane = pl.program_id(0)
    planes = pl.num_programs(0)
    sites = v_ref.shape[2]

    @pl.when(plane == 0)
    def _():
        acc[...] = jnp.zeros_like(acc)
        waves[...] = jnp.zeros_like(waves)
        vr[...] = jnp.zeros_like(vr)
        vz[...] = jnp.zeros_like(vz)
        f2[...] = jnp.zeros_like(f2)

    acc[2] += gram(f2, vz)
    vz[...] = vr[...]

    column = lax.broadcasted_iota(jnp.int32, (sites, sites), 1)
    row = lax.broadcasted_iota(jnp.int32, (sites, sites), 0)
    before = row - row % PX + (row + PX - 1) % PX
    permutation = jnp.where(column == before, 1.0, 0.0).astype(jnp.bfloat16)
    transposed_plane(v_ref, vt)
    stacked_plane(v_ref, vr)
    stacked_plane(v_ref, vy, PX)
    permuted_plane(v_ref, vx, permutation)

    u0 = u_ref[0].astype(jnp.float32)
    lane = lax.broadcasted_iota(jnp.int32, u0.shape, 3)
    link_sums(jnp.where(lane % PX == 0, turned(u0, sites - PX + 1), turned(u0, 1)), uf.at[0])
    link_sums(turned(u_ref[1].astype(jnp.float32), PX), uf.at[1])
    link_sums(below_ref[...].astype(jnp.float32), uf.at[2])

    direction(partial(link_rows, uf, (0,)), vt, f0)
    for part in range(2):
        for colour in range(3):
            vtb[part * LANES : (part + 1) * LANES, colour * sites : (colour + 1) * sites] = vt[
                3 * part + colour
            ].astype(jnp.bfloat16)
    own = dot(vtb[...], vr[...])
    g_real = block(own, 0, 0) + block(own, 1, 1)
    g_imag = block(own, 0, 1) - block(own, 1, 0)
    packed = jnp.where(upper(g_real.shape), g_real, g_imag)
    z = where_ref[1] * planes + plane
    angle = step * jnp.full((8, LANES), z, jnp.int32).astype(jnp.float32)
    waves[0] += jnp.cos(angle)[0:1] * packed
    waves[1] += jnp.sin(angle)[0:1] * packed

    acc[0] += gram(f0, vx)
    direction(partial(link_rows, uf, (1,)), vt, f1)
    acc[1] += gram(f1, vy)
    direction(partial(link_rows, uf, (2,)), vt, f2)

    @pl.when(plane == planes - 1)
    def _():
        parity = where_ref[1] % 2
        cos_sym, cos_anti = unpack(scale * waves[0])
        sin_sym, sin_anti = unpack(scale * waves[1])
        store_halves(out_ref, 0, antihermitian(acc[0], 0.5 * scale), parity)
        store_halves(out_ref, 1, antihermitian(acc[1], 0.5 * scale), parity)
        store_halves(out_ref, 2, cos_sym + sin_anti, parity)
        store_halves(out_ref, 3, cos_anti - sin_sym, parity)
        inner_ref[...] = antihermitian(acc[2] + gram(f2, vz), 0.5 * scale)


def rim_kernel(where_ref, v_ref, halo_ref, u_ref, inner_ref, out_ref, vt, vr, uf, f2, *, scale):
    link_sums(u_ref[...].astype(jnp.float32), uf)
    transposed_plane(halo_ref, vt)
    stacked_plane(v_ref, vr)
    direction(partial(link_rows, uf, ()), vt, f2)
    total = inner_ref[...] + antihermitian(gram(f2, vr), 0.5 * scale)
    store_halves(out_ref, 0, total, where_ref[1] % 2)


def unpack(packed):
    flipped = packed.T
    row = lax.broadcasted_iota(jnp.int32, packed.shape, 0)
    column = lax.broadcasted_iota(jnp.int32, packed.shape, 1)
    symmetric = jnp.where(row <= column, packed, flipped)
    antisymmetric = jnp.where(row > column, packed, jnp.where(row < column, -flipped, 0.0))
    return symmetric, antisymmetric


def round_kernel(mine_a, got_a, mine_b, got_b, out_ref):
    sums = mine_a[...] + got_a[...]
    out_ref[0] = sums[0].astype(jnp.bfloat16)
    out_ref[1] = sums[1].astype(jnp.bfloat16)
    out_ref[2] = (mine_b[0] + got_b[0]).astype(jnp.bfloat16)
    out_ref[3] = sums[2].astype(jnp.bfloat16)
    out_ref[4] = sums[3].astype(jnp.bfloat16)


def elemental(table, slot, code):
    third = code == 3
    packed = table[slot, jnp.where(third, 3, code)].astype(jnp.float32)
    other = table[slot, 4].astype(jnp.float32)
    symmetric, antisymmetric = unpack(packed)
    real = jnp.where(third, packed, antisymmetric)
    imag = jnp.where(third, other, symmetric)
    return real, imag


def fill(table, where_ref, parts):
    half_rows = table.shape[2] // 2
    parity = where_ref[1] % 2
    for at, halves in enumerate(parts):
        for i, half in enumerate(halves):
            start = pl.multiple_of((parity ^ i) * half_rows, half_rows)
            table[at, :, pl.ds(start, half_rows), :] = half[...]


def slot_of(where_ref, slice_index, tm_size):
    spin_size = where_ref[3]
    owner = slice_index // spin_size
    within = slice_index % spin_size
    return (within ^ where_ref[0]) * tm_size + (owner ^ where_ref[2])


def pair_kernel(where_ref, codes_ref, pairs_ref, operators_ref, *refs, tm_size, slots, q_count):
    *halves, tau_ref, out_ref, table = refs
    pair = pl.program_id(0)
    columns = LANES

    @pl.when(pair == 0)
    def _():
        fill(table, where_ref, [halves[i : i + 2] for i in range(0, len(halves), 2)])
        out_ref[...] = jnp.zeros_like(out_ref)

    def matrix(end):
        operator = operators_ref[end, pair]
        core = operator // slots
        code = codes_ref[(core ^ where_ref[0]) * slots + operator % slots]
        slot = slot_of(where_ref, pairs_ref[end, pair], tm_size)
        real, imag = elemental(table, slot, code)
        return real.astype(jnp.bfloat16), imag.astype(jnp.bfloat16)

    r_real, r_imag = matrix(0)
    s_real, s_imag = matrix(1)
    sink = jnp.concatenate(
        [
            jnp.concatenate([s_real, -s_imag], 1),
            jnp.concatenate([s_imag, s_real], 1),
        ],
        0,
    )
    source = jnp.concatenate(
        [
            jnp.concatenate([r_real, r_imag], 1),
            jnp.concatenate([-r_imag, r_real], 1),
        ],
        0,
    )
    sum_real = jnp.zeros((columns, columns), jnp.float32)
    sum_imag = jnp.zeros((columns, columns), jnp.float32)
    for q in range(0, q_count, 2):
        pairwise = jnp.concatenate(
            [tau_ref[q + i].reshape(2 * columns, columns) for i in range(2)], 1
        )
        halfway = dot(sink, pairwise)
        left = jnp.concatenate(
            [
                jnp.concatenate(
                    [
                        halfway[:columns, i * columns : (i + 1) * columns],
                        halfway[columns:, i * columns : (i + 1) * columns],
                    ],
                    1,
                )
                for i in range(2)
            ],
            0,
        )
        high = left.astype(jnp.bfloat16)
        low = (left - high.astype(jnp.float32)).astype(jnp.bfloat16)
        second = dot(high, source) + dot(low, source)
        for i in range(2):
            out_real = second[i * columns : (i + 1) * columns, :columns]
            out_imag = second[i * columns : (i + 1) * columns, columns:]
            tau_real = tau_ref[q + i, 0].astype(jnp.float32)
            tau_imag = tau_ref[q + i, 1].astype(jnp.float32)
            spin_pair = where_ref[0] * q_count + q + i
            sign = jnp.where((spin_pair // 4 < 2) == (spin_pair % 4 < 2), 1.0, -1.0)
            sum_real += sign * (out_real * tau_real + out_imag * tau_imag)
            sum_imag += sign * (out_imag * tau_real - out_real * tau_imag)
    total_real = jnp.sum(sum_real) / (4.0 * columns)
    total_imag = jnp.sum(sum_imag) / (4.0 * columns)
    row = lax.broadcasted_iota(jnp.int32, out_ref.shape, 0)
    column = lax.broadcasted_iota(jnp.int32, out_ref.shape, 1)
    total = jnp.where(row == 0, total_real, total_imag)
    out_ref[...] = jnp.where(column == pair, total, out_ref[...])


def elemental_kernel(where_ref, codes_ref, *refs):
    *halves, out_ref, table, rows_ref = refs
    fill(table, where_ref, [halves[i : i + 2] for i in range(0, len(halves), 2)])
    slices, slots, row_count = out_ref.shape[0], out_ref.shape[1], out_ref.shape[2]
    start = pl.multiple_of(where_ref[1] * row_count, row_count)
    for t in range(slices):
        for o in range(slots):
            real, imag = elemental(table, t ^ where_ref[0], codes_ref[o])
            rows_ref[0] = real
            rows_ref[1] = imag
            for part in range(2):
                out_ref[t, o, :, part] = rows_ref[part, pl.ds(start, row_count), :]


def shards(eigvecs, links, directions, pair_list, pair_operators, perambulators):
    slices, _, _, local_sites, columns = eigvecs.shape
    space = lax.axis_size("space")
    tm_size = lax.axis_size("tm")
    spin_size = lax.axis_size("spin")
    assert slices == spin_size and columns == LANES
    sites = PX * PY
    planes = local_sites // sites
    z_total = planes * space
    scale = 1.0 / math.sqrt(6.0 * sites * z_total)
    slots = directions.shape[0]
    pair_count, q_count = perambulators.shape[0], perambulators.shape[1]

    me = lax.axis_index("spin")
    where = jnp.stack(
        [me, lax.axis_index("space"), lax.axis_index("tm"), spin_size]
    ).astype(jnp.int32)
    lowest = lax.dynamic_slice(eigvecs, (me, 0, 0, 0, 0), (1, 2, 3, sites, columns))[0]
    halo = lax.ppermute(lowest, "space", [(i, (i - 1) % space) for i in range(space)])
    halo, other_codes = lax.optimization_barrier((halo, flip(directions, "spin", 1)))
    codes = jnp.concatenate([directions, other_codes])

    params = pltpu.CompilerParams(dimension_semantics=("arbitrary",), vmem_limit_bytes=50 << 20)
    stack_shape = pltpu.VMEM((3 * sites, 2 * LANES), jnp.bfloat16)
    f_shape = pltpu.VMEM((4 * LANES, 3 * sites), jnp.bfloat16)
    vt_shape = pltpu.VMEM((6, LANES, sites), jnp.float32)
    link_field = links.transpose(0, 1, 3, 4, 2, 5)
    estimate = lambda flops: pl.CostEstimate(flops=flops, bytes_accessed=1 << 22, transcendentals=0)
    half_rows = columns // 2
    part_a, inner = pl.pallas_call(
        partial(plane_kernel, scale=scale, step=2.0 * math.pi / z_total),
        out_shape=(
            jax.ShapeDtypeStruct((2, 4, half_rows, columns), jnp.float32),
            jax.ShapeDtypeStruct((columns, columns), jnp.float32),
        ),
        grid_spec=pltpu.PrefetchScalarGridSpec(
            num_scalar_prefetch=1,
            grid=(planes,),
            in_specs=[
                pl.BlockSpec((None, 2, 3, sites, columns), lambda z, w: (w[0], 0, 0, z, 0)),
                pl.BlockSpec((None, 2, 3, 3, 2, sites), lambda z, w: (w[0], 0, 0, 0, 0, z)),
                pl.BlockSpec(
                    (None, None, 3, 3, 2, sites),
                    lambda z, w: (w[0], 2, 0, 0, 0, jnp.maximum(z - 1, 0)),
                ),
            ],
            out_specs=(
                pl.BlockSpec((2, 4, half_rows, columns), lambda z, w: (0, 0, 0, 0)),
                pl.BlockSpec((columns, columns), lambda z, w: (0, 0)),
            ),
            scratch_shapes=[
                pltpu.VMEM((2, columns, columns), jnp.float32),
                vt_shape,
                pltpu.VMEM((2 * LANES, 3 * sites), jnp.bfloat16),
                stack_shape,
                stack_shape,
                stack_shape,
                stack_shape,
                pltpu.VMEM((3, 3, 3, 3, sites), jnp.float32),
                f_shape,
                f_shape,
                f_shape,
                pltpu.VMEM((3, 2 * LANES, 2 * LANES), jnp.float32),
            ],
        ),
        compiler_params=params,
        cost_estimate=estimate(20 * 10**9),
        name="planes",
    )(where, eigvecs, link_field, link_field)

    part_b = pl.pallas_call(
        partial(rim_kernel, scale=scale),
        out_shape=jax.ShapeDtypeStruct((2, 1, half_rows, columns), jnp.float32),
        grid_spec=pltpu.PrefetchScalarGridSpec(
            num_scalar_prefetch=1,
            grid=(1,),
            in_specs=[
                pl.BlockSpec((None, 2, 3, sites, columns), lambda z, w: (w[0], 0, 0, planes - 1, 0)),
                pl.BlockSpec((2, 3, sites, columns), lambda z, w: (0, 0, 0, 0)),
                pl.BlockSpec((None, None, 3, 3, 2, sites), lambda z, w: (w[0], 2, 0, 0, 0, planes - 1)),
                pl.BlockSpec((columns, columns), lambda z, w: (0, 0)),
            ],
            out_specs=pl.BlockSpec((2, 1, half_rows, columns), lambda z, w: (0, 0, 0, 0)),
            scratch_shapes=[
                vt_shape,
                stack_shape,
                pltpu.VMEM((3, 3, 3, sites), jnp.float32),
                f_shape,
            ],
        ),
        compiler_params=params,
        cost_estimate=estimate(2 * 10**9),
        name="rim",
    )(where, eigvecs, halo, link_field, inner)

    got_a = flip(part_a[1], "space", 1)
    got_b = flip(part_b[1], "space", 1)
    part_a, part_b = part_a[0], part_b[0]
    mask = 2
    while mask < space:
        part_a, got_a, part_b = lax.optimization_barrier((part_a, got_a, part_b))
        part_a, part_b = part_a + got_a, part_b + got_b
        got_a, got_b = flip(part_a, "space", mask), flip(part_b, "space", mask)
        mask *= 2

    mine = pl.pallas_call(
        round_kernel,
        out_shape=jax.ShapeDtypeStruct((5, half_rows, columns), jnp.bfloat16),
        compiler_params=pltpu.CompilerParams(vmem_limit_bytes=50 << 20),
        name="round",
    )(part_a, got_a, part_b, got_b)
    own = [mine, flip_both(mine, 1, 0)]
    for m in range(1, tm_size):
        own += [flip_both(mine, 0, m), flip_both(mine, 1, m)]
    other = [flip(half, "spin", 1) for half in own]

    whole = lambda shape: pl.BlockSpec(shape, lambda p, *_: (0,) * len(shape))

    row_count = columns // space
    elementals = pl.pallas_call(
        elemental_kernel,
        out_shape=jax.ShapeDtypeStruct((slices, slots, row_count, 2, columns), jnp.float32),
        grid_spec=pltpu.PrefetchScalarGridSpec(
            num_scalar_prefetch=2,
            grid=(1,),
            in_specs=[whole(mine.shape)] * 4,
            out_specs=whole((slices, slots, row_count, 2, columns)),
            scratch_shapes=[
                pltpu.VMEM((spin_size, 5, columns, columns), jnp.bfloat16),
                pltpu.VMEM((2, columns, columns), jnp.float32),
            ],
        ),
        compiler_params=params,
        name="rows",
    )(where, codes, *own[:2], *other[:2])

    partial_corr = pl.pallas_call(
        partial(pair_kernel, tm_size=tm_size, slots=slots, q_count=q_count),
        out_shape=jax.ShapeDtypeStruct((2, pair_count), jnp.float32),
        grid_spec=pltpu.PrefetchScalarGridSpec(
            num_scalar_prefetch=4,
            grid=(pair_count,),
            in_specs=[whole(mine.shape)] * (2 * len(own))
            + [
                pl.BlockSpec((None, q_count, 2, columns, columns), lambda p, *_: (p, 0, 0, 0, 0)),
            ],
            out_specs=whole((2, pair_count)),
            scratch_shapes=[
                pltpu.VMEM((spin_size * tm_size, 5, columns, columns), jnp.bfloat16)
            ],
        ),
        compiler_params=params,
        name="pairs",
    )(where, codes, pair_list.T, pair_operators.T, *own, *other, perambulators)
    correlators = (partial_corr + flip(partial_corr, "spin", 1)).T

    return elementals, correlators


def solution(mesh):
    return jax.shard_map(
        shards,
        mesh=mesh,
        in_specs=(
            P("tm", None, None, "space", None),
            P("tm", None, None, None, None, "space"),
            P("spin"),
            P(("space", "tm"), None),
            P(("space", "tm"), None),
            P(("space", "tm"), "spin", None, None, None),
        ),
        out_specs=(P(("ens", "tm"), "spin", "space", None, None), P(("ens", "space", "tm"), None)),
        check_vma=False,
    )
```

time: 296 us -> 58.9 us (0.20); the launches traced: 291 us -> 58.7 us
  waiting for transfers between devices: 113 us -> 13.6 us
  other arithmetic: 58.5 us -> 0.74 us
  local copies, waits for them, and re-layouts: 55.9 us -> 2.1 us
  loops' own time: 28.3 us -> 0 us
  Pallas kernels: 0 us -> 27.4 us
  between operations: 15.8 us -> 0.76 us
  matrix products: 8.55 us -> 0 us
  starting transfers between devices: 7.01 us -> 14 us
  blocking collectives: 3.01 us -> 0 us
    psum x1 -> x0, waiting for transfers between devices: 69.8 us -> none  [shards(): totals = lax.psum(partials, 'space')]
    another operation x6 -> x0, loops' own time: 28.3 us -> none  [the longest x4 24.9 us: per_slice(): lax.switch(directions[op_slot], branches, vectors, link_field, upper_rim,...]
    pallas_call x0 -> x5, Pallas kernels: none -> 27.4 us  [the longest x1 18.5 us: shards(): pl.pallas_call(partial(plane_kernel, scale=scale, step=2.0 * math.pi / z_...]
    add x6 -> x2, other arithmetic: 20.8 us -> 0.02 us  [shards(): part_a, part_b = (part_a + got_a, part_b + got_b)]
    ppermute x3 -> x14, waiting for transfers between devices: 28.7 us -> 13.6 us  [the longest x10 9.73 us: flip(): return lax.ppermute(array, axis, [(i, i ^ mask) for i in range(count)])]
    all_gather x1 -> x0, waiting for transfers between devices: 14.9 us -> none  [shards(): lax.all_gather(totals.astype(jnp.bfloat16)[None], ('tm', 'spin'), axis=0,...]
    dynamic_slice x11 -> x0, local copies, waits for them, and re-layouts: 14.5 us -> none  [the longest x6 9.22 us: shards(): partials = lax.map(per_slice, (eigvecs, links, plane_above, plane_below))]
    convert_element_type x12 -> x0, other arithmetic: 14.2 us -> none  [the longest x2 7.38 us: per_slice(): vectors_half.astype(jnp.float32).reshape(2, 3, plane_count, PY, PX, columns)]
  transfers between devices with their start and end apart: 5 -> 14, of which waited for: 4 -> 7; matrix products, arithmetic and copies ran while one was open for 3% -> 0% of each run, Pallas kernels for 0% -> 38%
where the time goes in v1:
time: 58.9 us; the launch traced here: 58.7 us
  Pallas kernels  27.4 us (47%)
  starting transfers between devices  14 us (24%)
  waiting for transfers between devices  13.6 us (23%)
  local copies, waits for them, and re-layouts  2.1 us (4%)
  between operations  0.76 us (1%)
  other arithmetic  0.74 us (1%)
    pallas_call x1, Pallas kernels, shards(): pl.pallas_call(partial(plane_kernel, scale=scale, step=2.0 * math.pi / z_...  18.5 us
    ppermute x10, waiting for transfers between devices, flip(): return lax.ppermute(array, axis, [(i, i ^ mask) for i in range(count)])  9.73 us
    ppermute x10, starting transfers between devices, flip(): return lax.ppermute(array, axis, [(i, i ^ mask) for i in range(count)])  5.36 us
    ppermute x1, starting transfers between devices, shards(): lax.ppermute(lowest, 'space', [(i, (i - 1) % space) for i in range(space)])  5.13 us
    pallas_call x1, Pallas kernels, shards(): pl.pallas_call(partial(pair_kernel, tm_size=tm_size, slots=slots, q_count...  4.97 us
    ppermute x3, waiting for transfers between devices, flip_both(): return lax.ppermute(array, ('space', 'tm'), pairs)  3.87 us
    ppermute x3, starting transfers between devices, flip_both(): return lax.ppermute(array, ('space', 'tm'), pairs)  3.55 us
    pallas_call x1, Pallas kernels, shards(): pl.pallas_call(partial(rim_kernel, scale=scale), out_shape=jax.ShapeDtype...  2.47 us
  transfers between devices with their start and end apart: 14, of which 7 were waited for; matrix products, arithmetic and copies ran while one was open for 0% of the time, Pallas kernels for 38%

profile of v1, /device:TPU:0, one launch (start us, length us, event | category | flops | bytes accessed | tf_op | source)
XLA Modules:
  0.0 58.7 jit_solution(9721137547782165753)
XLA Ops:
  0.6 1.0 %dynamic-slice_bitcast_fusion = bf16[2,3,256,128]{3,2,1,0:T(8,128)(2,1)S(1)} fusion(bf16[2,2,3,2048,128]{4,3,2,1,0:T(8,128)(2,1)} %v_ref.3, s32[]{:T(128)S(6)} %select_n.3), kind=kLoop, calls=%fused_computation | loop fusion | bytes 786436 | tf_op jit(solution)/shard_map/squeeze | solution.py:360
  1.7 5.1 %collective-permute-start = (bf16[2,3,256,128]{3,2,1,0:T(8,128)(2,1)S(1)}, bf16[2,3,256,128]{3,2,1,0:T(8,128)(2,1)S(1)}, u32[]{:S(2)}, u32[]{:S(2)}) collective-permute-start(bf16[2,3,256,128]{3,2,1,0:T(8,128)(2,1)S(1)} %dynamic-slice_bitcast_fusion), channel_id=1, source_target_pairs={{0,12},{4,0},{8,4},{12,8},{1,13},{5,1},{9,5},{13,9},{2,14},{6,2},{... | collective-permute-start | bytes 1179656 | tf_op jit(solution)/shard_map/ppermute | solution.py:361
  6.8 0.0 collective-permute-start.1
  6.8 0.1 pad_add_fusion.where_ref
  6.9 0.0 copy-start.3
  6.9 1.0 %copy-done.3 = bf16[2,3,2,3,3,2048]{5,2,4,3,1,0:T(2,128)(2,1)S(1)} copy-done((bf16[2,3,2,3,3,2048]{5,2,4,3,1,0:T(2,128)(2,1)S(1)}, bf16[2,3,2,3,3,2048]{5,2,4,3,1,0:T(2,128)(2,1)}, u32[]{:S(2)}) %copy-start.3) | copy-done | bytes 442392
  7.9 18.5 %planes.1 = (f32[2,4,64,128]{3,2,1,0:T(8,128)S(1)}, f32[128,128]{1,0:T(8,128)S(1)}) custom-call(s32[4]{0:T(128)S(1)} %pad_add_fusion.where_ref, bf16[2,2,3,2048,128]{4,3,2,1,0:T(8,128)(2,1)} %v_ref.3, bf16[2,3,3,3,2,2048]{5,4,3,2,1,0:T(2,128)(2,1)S(1)} %bitcast.20, bf16[2,3,3,3,2,2048]{5,4,3,2,1,0:T(2,128)(2,1)S(1)} %bitcast.21), custom_call_target="tpu_custom_call" | custom-call | flops 20000000000 | bytes 4194304 | tf_op jit(solution)/shard_map/planes/pallas_call | solution.py:372
  26.4 0.0 copy-start.4
  26.4 0.0 copy-start
  26.4 0.0 copy-start.1
  26.4 0.0 copy-start.2
  26.5 0.1 collective-permute-start.2
  26.6 0.0 collective-permute-done.1
  26.6 0.0 collective-permute-done.halo_ref
  26.6 2.5 %rim.1 = f32[2,1,64,128]{3,2,1,0:T(8,128)S(1)} custom-call(s32[4]{0:T(128)S(1)} %pad_add_fusion.where_ref, bf16[2,2,3,2048,128]{4,3,2,1,0:T(8,128)(2,1)} %v_ref.3, bf16[2,3,256,128]{3,2,1,0:T(8,128)(2,1)S(1)} %collective-permute-done.halo_ref, bf16[2,3,3,3,2,2048]{5,4,3,2,1,0:T(2,128)(2,1)S(1)} %bitcast.22, f32[128,128]{1,0:T(8,128)S(1)} %get-tuple-element.12.inner_ref), custom_call_target="tpu_custom_call" | custom-call | flops 2000000000 | bytes 4194304 | tf_op jit(solution)/shard_map/rim/pallas_call | solution.py:413
  29.1 3.4 %collective-permute-done.2 = f32[4,64,128]{2,1,0:T(8,128)S(1)} collective-permute-done((f32[4,64,128]{2,1,0:T(8,128)S(1)}, f32[4,64,128]{2,1,0:T(8,128)S(1)}, u32[]{:S(2)}, u32[]{:S(2)}) %collective-permute-start.2) | collective-permute-done | bytes 131104 | tf_op jit(solution)/shard_map/ppermute | solution.py:19
  32.5 0.1 collective-permute-start.3
  32.5 1.0 %collective-permute-start.4 = (f32[1,64,128]{2,1,0:T(8,128)S(1)}, f32[1,64,128]{2,1,0:T(8,128)S(1)}, u32[]{:S(2)}, u32[]{:S(2)}) collective-permute-start(f32[1,64,128]{2,1,0:T(8,128)S(1)} %get-tuple-element.18), channel_id=1, source_target_pairs={{0,4},{4,0},{8,12},{12,8},{1,5},{5,1},{9,13},{13,9},{2,6},{6,2},{1... | collective-permute-start | bytes 98312 | tf_op jit(solution)/shard_map/ppermute | solution.py:19
  33.6 3.0 %collective-permute-done.4 = f32[1,64,128]{2,1,0:T(8,128)S(1)} collective-permute-done((f32[1,64,128]{2,1,0:T(8,128)S(1)}, f32[1,64,128]{2,1,0:T(8,128)S(1)}, u32[]{:S(2)}, u32[]{:S(2)}) %collective-permute-start.4) | collective-permute-done | bytes 32800 | tf_op jit(solution)/shard_map/ppermute | solution.py:19
  36.5 3.3 %collective-permute-start.5 = (f32[1,64,128]{2,1,0:T(8,128)S(1)}, f32[1,64,128]{2,1,0:T(8,128)S(1)}, u32[]{:S(2)}, u32[]{:S(2)}) collective-permute-start(f32[1,64,128]{2,1,0:T(8,128)S(1)} %add.14.mine_b), channel_id=1, source_target_pairs={{0,8},{4,12},{8,0},{12,4},{1,9},{5,13},{9,1},{13,5},{2,10},{6,14},... | collective-permute-start | bytes 98312 | tf_op jit(solution)/shard_map/ppermute | solution.py:19
  39.8 2.5 %collective-permute-done.5.got_b = f32[1,64,128]{2,1,0:T(8,128)S(1)} collective-permute-done((f32[1,64,128]{2,1,0:T(8,128)S(1)}, f32[1,64,128]{2,1,0:T(8,128)S(1)}, u32[]{:S(2)}, u32[]{:S(2)}) %collective-permute-start.5) | collective-permute-done | bytes 32800 | tf_op jit(solution)/shard_map/ppermute | solution.py:19
  42.3 0.0 collective-permute-done.3.got_a
  42.4 1.6 %collective-permute-start.9 = (bf16[5,64,128]{2,1,0:T(8,128)(2,1)S(1)}, bf16[5,64,128]{2,1,0:T(8,128)(2,1)S(1)}, u32[]{:S(2)}, u32[]{:S(2)}) collective-permute-start(bf16[5,64,128]{2,1,0:T(8,128)(2,1)S(1)} %round.1.refs_0_), channel_id=1, source_target_pairs={{0,2},{2,0},{4,6},{6,4},{8,10},{10,8},{12,14},{14,12},{1,3},{3,1},... | collective-permute-start | bytes 245768 | tf_op jit(solution)/shard_map/ppermute | solution.py:27
  43.9 1.0 %collective-permute-start.10 = (bf16[5,64,128]{2,1,0:T(8,128)(2,1)S(1)}, bf16[5,64,128]{2,1,0:T(8,128)(2,1)S(1)}, u32[]{:S(2)}, u32[]{:S(2)}) collective-permute-start(bf16[5,64,128]{2,1,0:T(8,128)(2,1)S(1)} %round.1.refs_0_), channel_id=1, source_target_pairs={{0,6},{2,4},{4,2},{6,0},{8,14},{10,12},{12,10},{14,8},{1,7},{3,5},... | collective-permute-start | bytes 245768 | tf_op jit(solution)/shard_map/ppermute | solution.py:27
  45.0 0.9 %collective-permute-start.6 = (bf16[5,64,128]{2,1,0:T(8,128)(2,1)S(1)}, bf16[5,64,128]{2,1,0:T(8,128)(2,1)S(1)}, u32[]{:S(2)}, u32[]{:S(2)}) collective-permute-start(bf16[5,64,128]{2,1,0:T(8,128)(2,1)S(1)} %round.1.refs_0_), channel_id=1, source_target_pairs={{0,4},{2,6},{4,0},{6,2},{8,12},{10,14},{12,8},{14,10},{1,5},{3,7},... | collective-permute-start | bytes 245768 | tf_op jit(solution)/shard_map/ppermute | solution.py:27
  45.9 0.0 collective-permute-start.7
  45.9 1.0 %collective-permute-done.9.refs_2_ = bf16[5,64,128]{2,1,0:T(8,128)(2,1)S(1)} collective-permute-done((bf16[5,64,128]{2,1,0:T(8,128)(2,1)S(1)}, bf16[5,64,128]{2,1,0:T(8,128)(2,1)S(1)}, u32[]{:S(2)}, u32[]{:S(2)}) %collective-permute-start.9) | collective-permute-done | bytes 81952 | tf_op jit(solution)/shard_map/ppermute | solution.py:27
  47.0 0.0 collective-permute-start.11
  47.0 2.8 %collective-permute-done.10.refs_3_ = bf16[5,64,128]{2,1,0:T(8,128)(2,1)S(1)} collective-permute-done((bf16[5,64,128]{2,1,0:T(8,128)(2,1)S(1)}, bf16[5,64,128]{2,1,0:T(8,128)(2,1)S(1)}, u32[]{:S(2)}, u32[]{:S(2)}) %collective-permute-start.10) | collective-permute-done | bytes 81952 | tf_op jit(solution)/shard_map/ppermute | solution.py:27
  49.8 0.0 collective-permute-start.12
  49.8 0.0 collective-permute-done.6.refs_1_
  49.8 0.5 collective-permute-start.8
  50.3 0.0 copy-done.4
  50.3 0.1 pad_add_fusion.1.codes_ref
  50.4 0.0 collective-permute-done.7.refs_2_.refs_4_
  50.4 0.0 collective-permute-done.11.refs_6_
  50.4 0.7 %collective-permute-done.12.refs_7_ = bf16[5,64,128]{2,1,0:T(8,128)(2,1)S(1)} collective-permute-done((bf16[5,64,128]{2,1,0:T(8,128)(2,1)S(1)}, bf16[5,64,128]{2,1,0:T(8,128)(2,1)S(1)}, u32[]{:S(2)}, u32[]{:S(2)}) %collective-permute-start.12) | collective-permute-done | bytes 81952 | tf_op jit(solution)/shard_map/ppermute | solution.py:19
  51.1 0.2 collective-permute-done.8.refs_3_.refs_5_
  51.2 0.0 copy-done
  51.2 0.0 copy-done.1
  51.2 0.0 copy-done.2
  51.2 5.0 %pairs.1 = f32[2,4]{1,0:T(2,128)S(1)} custom-call(s32[4]{0:T(128)S(1)} %pad_add_fusion.where_ref, s32[4]{0:T(128)S(1)} %pad_add_fusion.1.codes_ref, s32[2,4]{1,0:T(2,128)S(1)} %bitcast.18, s32[2,4]{1,0:T(2,128)S(1)} %bitcast.19, bf16[5,64,128]{2,1,0:T(8,128)(2,1)S(1)} %round.1.refs_0_, bf16[5,64,128]{2,1,0:T(8,128)(2,1)S(1)} %collective-permute-done.6.refs_1_, ...), custom_call_target="tpu_custom_call" | custom-call | tf_op jit(solution)/shard_map/pairs/pallas_call | solution.py:479
  56.2 0.4 collective-permute-start.13
  56.6 1.5 %rows.1 = f32[2,2,32,2,128]{4,3,2,1,0:T(2,128)} custom-call(s32[4]{0:T(128)S(1)} %pad_add_fusion.where_ref, s32[4]{0:T(128)S(1)} %pad_add_fusion.1.codes_ref, bf16[5,64,128]{2,1,0:T(8,128)(2,1)S(1)} %round.1.refs_0_, bf16[5,64,128]{2,1,0:T(8,128)(2,1)S(1)} %collective-permute-done.6.refs_1_, bf16[5,64,128]{2,1,0:T(8,128)(2,1)S(1)} %collective-permute-done.7.refs_2_.refs_4_, ...), custom_call_target="tpu_custom_call" | custom-call | tf_op jit(solution)/shard_map/rows/pallas_call | solution.py:462
  58.1 0.0 collective-permute-done.13
  58.1 0.6 add_bitcast_fusion
  (5 shorter events, 0.1 us)
Async XLA Ops:
  1.7 24.9 %collective-permute-start = (bf16[2,3,256,128]{3,2,1,0:T(8,128)(2,1)S(1)}, bf16[2,3,256,128]{3,2,1,0:T(8,128)(2,1)S(1)}, u32[]{:S(2)}, u32[]{:S(2)}) collective-permute-start(bf16[2,3,256,128]{3,2,1,0:T(8,128)(2,1)S(1)} %dynamic-slice_bitcast_fusion), channel_id=1, source_target_pairs={{0,12},{4,0},{8,4},{12,8},{1,13},{5,1},{9,5},{13,9},{2,14},{6,2},{... | collective-permute-start | bytes 1179656 | tf_op jit(solution)/shard_map/ppermute | solution.py:361
  6.8 19.8 %collective-permute-start.1 = (s32[2]{0:T(128)}, s32[2]{0:T(128)S(1)}, u32[]{:S(2)}, u32[]{:S(2)}) collective-permute-start(s32[2]{0:T(128)} %param.8), channel_id=1, source_target_pairs={{0,1},{1,0},{2,3},{3,2},{4,5},{5,4},{6,7},{7,6},{8,9},{9,8},{10,11... | collective-permute-start | bytes 32 | tf_op jit(solution)/shard_map/ppermute | solution.py:19
  6.9 1.0 %copy-start.3 = (bf16[2,3,2,3,3,2048]{5,2,4,3,1,0:T(2,128)(2,1)S(1)}, bf16[2,3,2,3,3,2048]{5,2,4,3,1,0:T(2,128)(2,1)}, u32[]{:S(2)}) copy-start(bf16[2,3,2,3,3,2048]{5,2,4,3,1,0:T(2,128)(2,1)} %param.7) | copy-start | bytes 1327108
  26.4 23.9 %copy-start.4 = (s32[2]{0:T(128)S(1)}, s32[2]{0:T(128)}, u32[]{:S(2)}) copy-start(s32[2]{0:T(128)} %param.8) | copy-start | bytes 28
  26.4 24.8 %copy-start = (bf16[4,8,2,128,128]{4,3,2,1,0:T(8,128)(2,1)S(1)}, bf16[4,8,2,128,128]{4,3,2,1,0:T(8,128)(2,1)}, u32[]{:S(2)}) copy-start(bf16[4,8,2,128,128]{4,3,2,1,0:T(8,128)(2,1)} %refs_8_.1) | copy-start | bytes 6291460
  26.4 24.8 %copy-start.1 = (s32[4,2]{0,1:T(2,128)S(1)}, s32[4,2]{0,1:T(2,128)}, u32[]{:S(2)}) copy-start(s32[4,2]{0,1:T(2,128)} %param.9) | copy-start | bytes 100
  26.4 24.8 %copy-start.2 = (s32[4,2]{0,1:T(2,128)S(1)}, s32[4,2]{0,1:T(2,128)}, u32[]{:S(2)}) copy-start(s32[4,2]{0,1:T(2,128)} %param.10) | copy-start | bytes 100
  26.5 6.0 %collective-permute-start.2 = (f32[4,64,128]{2,1,0:T(8,128)S(1)}, f32[4,64,128]{2,1,0:T(8,128)S(1)}, u32[]{:S(2)}, u32[]{:S(2)}) collective-permute-start(f32[4,64,128]{2,1,0:T(8,128)S(1)} %get-tuple-element.16), channel_id=1, source_target_pairs={{0,4},{4,0},{8,12},{12,8},{1,5},{5,1},{9,13},{13,9},{2,6},{6,2},{1... | collective-permute-start | bytes 393224 | tf_op jit(solution)/shard_map/ppermute | solution.py:19
  32.5 9.9 %collective-permute-start.3 = (f32[4,64,128]{2,1,0:T(8,128)S(1)}, f32[4,64,128]{2,1,0:T(8,128)S(1)}, u32[]{:S(2)}, u32[]{:S(2)}) collective-permute-start(f32[4,64,128]{2,1,0:T(8,128)S(1)} %add.13.mine_a), channel_id=1, source_target_pairs={{0,8},{4,12},{8,0},{12,4},{1,9},{5,13},{9,1},{13,5},{2,10},{6,14},... | collective-permute-start | bytes 393224 | tf_op jit(solution)/shard_map/ppermute | solution.py:19
  32.5 4.0 %collective-permute-start.4 = (f32[1,64,128]{2,1,0:T(8,128)S(1)}, f32[1,64,128]{2,1,0:T(8,128)S(1)}, u32[]{:S(2)}, u32[]{:S(2)}) collective-permute-start(f32[1,64,128]{2,1,0:T(8,128)S(1)} %get-tuple-element.18), channel_id=1, source_target_pairs={{0,4},{4,0},{8,12},{12,8},{1,5},{5,1},{9,13},{13,9},{2,6},{6,2},{1... | collective-permute-start | bytes 98312 | tf_op jit(solution)/shard_map/ppermute | solution.py:19
  36.5 5.8 %collective-permute-start.5 = (f32[1,64,128]{2,1,0:T(8,128)S(1)}, f32[1,64,128]{2,1,0:T(8,128)S(1)}, u32[]{:S(2)}, u32[]{:S(2)}) collective-permute-start(f32[1,64,128]{2,1,0:T(8,128)S(1)} %add.14.mine_b), channel_id=1, source_target_pairs={{0,8},{4,12},{8,0},{12,4},{1,9},{5,13},{9,1},{13,5},{2,10},{6,14},... | collective-permute-start | bytes 98312 | tf_op jit(solution)/shard_map/ppermute | solution.py:19
  42.4 4.6 %collective-permute-start.9 = (bf16[5,64,128]{2,1,0:T(8,128)(2,1)S(1)}, bf16[5,64,128]{2,1,0:T(8,128)(2,1)S(1)}, u32[]{:S(2)}, u32[]{:S(2)}) collective-permute-start(bf16[5,64,128]{2,1,0:T(8,128)(2,1)S(1)} %round.1.refs_0_), channel_id=1, source_target_pairs={{0,2},{2,0},{4,6},{6,4},{8,10},{10,8},{12,14},{14,12},{1,3},{3,1},... | collective-permute-start | bytes 245768 | tf_op jit(solution)/shard_map/ppermute | solution.py:27
  43.9 5.9 %collective-permute-start.10 = (bf16[5,64,128]{2,1,0:T(8,128)(2,1)S(1)}, bf16[5,64,128]{2,1,0:T(8,128)(2,1)S(1)}, u32[]{:S(2)}, u32[]{:S(2)}) collective-permute-start(bf16[5,64,128]{2,1,0:T(8,128)(2,1)S(1)} %round.1.refs_0_), channel_id=1, source_target_pairs={{0,6},{2,4},{4,2},{6,0},{8,14},{10,12},{12,10},{14,8},{1,7},{3,5},... | collective-permute-start | bytes 245768 | tf_op jit(solution)/shard_map/ppermute | solution.py:27
  45.0 4.8 %collective-permute-start.6 = (bf16[5,64,128]{2,1,0:T(8,128)(2,1)S(1)}, bf16[5,64,128]{2,1,0:T(8,128)(2,1)S(1)}, u32[]{:S(2)}, u32[]{:S(2)}) collective-permute-start(bf16[5,64,128]{2,1,0:T(8,128)(2,1)S(1)} %round.1.refs_0_), channel_id=1, source_target_pairs={{0,4},{2,6},{4,0},{6,2},{8,12},{10,14},{12,8},{14,10},{1,5},{3,7},... | collective-permute-start | bytes 245768 | tf_op jit(solution)/shard_map/ppermute | solution.py:27
  45.9 4.5 %collective-permute-start.7 = (bf16[5,64,128]{2,1,0:T(8,128)(2,1)S(1)}, bf16[5,64,128]{2,1,0:T(8,128)(2,1)S(1)}, u32[]{:S(2)}, u32[]{:S(2)}) collective-permute-start(bf16[5,64,128]{2,1,0:T(8,128)(2,1)S(1)} %round.1.refs_0_), channel_id=1, source_target_pairs={{0,1},{1,0},{2,3},{3,2},{4,5},{5,4},{6,7},{7,6},{8,9},{9,8},{10,11... | collective-permute-start | bytes 245768 | tf_op jit(solution)/shard_map/ppermute | solution.py:19
  47.0 3.4 %collective-permute-start.11 = (bf16[5,64,128]{2,1,0:T(8,128)(2,1)S(1)}, bf16[5,64,128]{2,1,0:T(8,128)(2,1)S(1)}, u32[]{:S(2)}, u32[]{:S(2)}) collective-permute-start(bf16[5,64,128]{2,1,0:T(8,128)(2,1)S(1)} %collective-permute-done.9.refs_2_), channel_id=1, source_target_pairs={{0,1},{1,0},{2,3},{3,2},{4,5},{5,4},{6,7},{7,6},{8,9},{9,8},{10,11... | collective-permute-start | bytes 245768 | tf_op jit(solution)/shard_map/ppermute | solution.py:19
  49.8 1.3 %collective-permute-start.12 = (bf16[5,64,128]{2,1,0:T(8,128)(2,1)S(1)}, bf16[5,64,128]{2,1,0:T(8,128)(2,1)S(1)}, u32[]{:S(2)}, u32[]{:S(2)}) collective-permute-start(bf16[5,64,128]{2,1,0:T(8,128)(2,1)S(1)} %collective-permute-done.10.refs_3_), channel_id=1, source_target_pairs={{0,1},{1,0},{2,3},{3,2},{4,5},{5,4},{6,7},{7,6},{8,9},{9,8},{10,11... | collective-permute-start | bytes 245768 | tf_op jit(solution)/shard_map/ppermute | solution.py:19
  49.8 1.4 %collective-permute-start.8 = (bf16[5,64,128]{2,1,0:T(8,128)(2,1)S(1)}, bf16[5,64,128]{2,1,0:T(8,128)(2,1)S(1)}, u32[]{:S(2)}, u32[]{:S(2)}) collective-permute-start(bf16[5,64,128]{2,1,0:T(8,128)(2,1)S(1)} %collective-permute-done.6.refs_1_), channel_id=1, source_target_pairs={{0,1},{1,0},{2,3},{3,2},{4,5},{5,4},{6,7},{7,6},{8,9},{9,8},{10,11... | collective-permute-start | bytes 245768 | tf_op jit(solution)/shard_map/ppermute | solution.py:19
  56.2 1.9 %collective-permute-start.13 = (f32[2,4]{1,0:T(2,128)S(1)}, f32[2,4]{1,0:T(2,128)S(1)}, u32[]{:S(2)}, u32[]{:S(2)}) collective-permute-start(f32[2,4]{1,0:T(2,128)S(1)} %pairs.1), channel_id=1, source_target_pairs={{0,1},{1,0},{2,3},{3,2},{4,5},{5,4},{6,7},{7,6},{8,9},{9,8},{10,11... | collective-permute-start | bytes 104 | tf_op jit(solution)/shard_map/ppermute | solution.py:19

commit v2 on v1

--- a/solution.py
+++ b/solution.py
@@ -250,6 +250,10 @@
     owner = slice_index // spin_size
     within = slice_index % spin_size
     return (within ^ where_ref[0]) * tm_size + (owner ^ where_ref[2])
+
+
+def folded(values):
+    return jnp.sum(values.reshape(-1, 8, values.shape[1]), axis=0)
 
 
 def pair_kernel(where_ref, codes_ref, pairs_ref, operators_ref, *refs, tm_size, slots, q_count):
@@ -286,8 +290,9 @@
         ],
         0,
     )
-    sum_real = jnp.zeros((columns, columns), jnp.float32)
-    sum_imag = jnp.zeros((columns, columns), jnp.float32)
+    twice = jnp.concatenate([source, source], 0)
+    sum_real = jnp.zeros((8, columns), jnp.float32)
+    sum_imag = jnp.zeros((8, columns), jnp.float32)
     for q in range(0, q_count, 2):
         pairwise = jnp.concatenate(
             [tau_ref[q + i].reshape(2 * columns, columns) for i in range(2)], 1
@@ -308,7 +313,7 @@
         )
         high = left.astype(jnp.bfloat16)
         low = (left - high.astype(jnp.float32)).astype(jnp.bfloat16)
-        second = dot(high, source) + dot(low, source)
+        second = dot(jnp.concatenate([high, low], 1), twice)
         for i in range(2):
             out_real = second[i * columns : (i + 1) * columns, :columns]
             out_imag = second[i * columns : (i + 1) * columns, columns:]
@@ -316,8 +321,8 @@
             tau_imag = tau_ref[q + i, 1].astype(jnp.float32)
             spin_pair = where_ref[0] * q_count + q + i
             sign = jnp.where((spin_pair // 4 < 2) == (spin_pair % 4 < 2), 1.0, -1.0)
-            sum_real += sign * (out_real * tau_real + out_imag * tau_imag)
-            sum_imag += sign * (out_imag * tau_real - out_real * tau_imag)
+            sum_real += sign * folded(out_real * tau_real + out_imag * tau_imag)
+            sum_imag += sign * folded(out_imag * tau_real - out_real * tau_imag)
     total_real = jnp.sum(sum_real) / (4.0 * columns)
     total_imag = jnp.sum(sum_imag) / (4.0 * columns)
     row = lax.broadcasted_iota(jnp.int32, out_ref.shape, 0)
@@ -366,7 +371,9 @@
     stack_shape = pltpu.VMEM((3 * sites, 2 * LANES), jnp.bfloat16)
     f_shape = pltpu.VMEM((4 * LANES, 3 * sites), jnp.bfloat16)
     vt_shape = pltpu.VMEM((6, LANES, sites), jnp.float32)
-    link_field = links.transpose(0, 1, 3, 4, 2, 5)
+    link_field = pltpu.with_memory_space_constraint(
+        links.transpose(0, 1, 3, 4, 2, 5), pltpu.MemorySpace.HBM
+    )
     estimate = lambda flops: pl.CostEstimate(flops=flops, bytes_accessed=1 << 22, transcendentals=0)
     half_rows = columns // 2
     part_a, inner = pl.pallas_call(
@@ -454,7 +461,7 @@
     own = [mine, flip_both(mine, 1, 0)]
     for m in range(1, tm_size):
         own += [flip_both(mine, 0, m), flip_both(mine, 1, m)]
-    other = [flip(half, "spin", 1) for half in own]
+    other = [flip(half, "spin", 1) for half in own[:2]]
 
     whole = lambda shape: pl.BlockSpec(shape, lambda p, *_: (0,) * len(shape))
 
@@ -474,7 +481,10 @@
         ),
         compiler_params=params,
         name="rows",
-    )(where, codes, *own[:2], *other[:2])
+    )(where, codes, *own[:2], *other)
+    *rest, elementals = lax.optimization_barrier((*own[2:], elementals))
+    own = own[:2] + rest
+    other = other + [flip(half, "spin", 1) for half in rest]
 
     partial_corr = pl.pallas_call(
         partial(pair_kernel, tm_size=tm_size, slots=slots, q_count=q_count),

time: 58.9 us -> 57.8 us (0.981)
  local copies, waits for them, and re-layouts: 2.1 us -> 1.08 us
    ppermute x10, waiting for transfers between devices: 9.73 us -> 11.8 us  [flip(): return lax.ppermute(array, axis, [(i, i ^ mask) for i in range(count)])]
    ppermute x3, waiting for transfers between devices: 3.87 us -> 1.82 us  [flip_both(): return lax.ppermute(array, ('space', 'tm'), pairs)]
    unnamed x10 -> x8, local copies, waits for them, and re-layouts: 1.04 us -> 0.03 us
  transfers between devices with their start and end apart: 14 -> 14, of which waited for: 7 -> 9; matrix products, arithmetic and copies ran while one was open for 0% -> 0% of each run, Pallas kernels for 38% -> 39%
where the time goes in v2:
time: 57.8 us; the launch traced here: 57.6 us
  Pallas kernels  27.4 us (47%)
  starting transfers between devices  14 us (24%)
  waiting for transfers between devices  13.7 us (24%)
  local copies, waits for them, and re-layouts  1.08 us (2%)
  between operations  0.76 us (1%)
  other arithmetic  0.74 us (1%)
    pallas_call x1, Pallas kernels, shards(): pl.pallas_call(partial(plane_kernel, scale=scale, step=2.0 * math.pi / z_...  18.5 us
    ppermute x10, waiting for transfers between devices, flip(): return lax.ppermute(array, axis, [(i, i ^ mask) for i in range(count)])  11.8 us
    ppermute x10, starting transfers between devices, flip(): return lax.ppermute(array, axis, [(i, i ^ mask) for i in range(count)])  5.35 us
    ppermute x1, starting transfers between devices, shards(): lax.ppermute(lowest, 'space', [(i, (i - 1) % space) for i in range(space)])  5.13 us
    pallas_call x1, Pallas kernels, shards(): pl.pallas_call(partial(pair_kernel, tm_size=tm_size, slots=slots, q_count...  4.91 us
    ppermute x3, starting transfers between devices, flip_both(): return lax.ppermute(array, ('space', 'tm'), pairs)  3.55 us
    pallas_call x1, Pallas kernels, shards(): pl.pallas_call(partial(rim_kernel, scale=scale), out_shape=jax.ShapeDtype...  2.48 us
    ppermute x3, waiting for transfers between devices, flip_both(): return lax.ppermute(array, ('space', 'tm'), pairs)  1.82 us
  transfers between devices with their start and end apart: 14, of which 9 were waited for; matrix products, arithmetic and copies ran while one was open for 0% of the time, Pallas kernels for 39%

profile of v2, /device:TPU:0, one launch (start us, length us, event | category | flops | bytes accessed | tf_op | source)
XLA Modules:
  0.0 57.6 jit_solution(14912175835182334827)
XLA Ops:
  0.6 1.0 %dynamic-slice_bitcast_fusion = bf16[2,3,256,128]{3,2,1,0:T(8,128)(2,1)S(1)} fusion(bf16[2,2,3,2048,128]{4,3,2,1,0:T(8,128)(2,1)} %v_ref.3, s32[]{:T(128)S(6)} %select_n.3), kind=kLoop, calls=%fused_computation | loop fusion | bytes 786436 | tf_op jit(solution)/shard_map/squeeze | solution.py:365
  1.7 5.1 %collective-permute-start.1 = (bf16[2,3,256,128]{3,2,1,0:T(8,128)(2,1)S(1)}, bf16[2,3,256,128]{3,2,1,0:T(8,128)(2,1)S(1)}, u32[]{:S(2)}, u32[]{:S(2)}) collective-permute-start(bf16[2,3,256,128]{3,2,1,0:T(8,128)(2,1)S(1)} %dynamic-slice_bitcast_fusion), channel_id=1, source_target_pairs={{0,12},{4,0},{8,4},{12,8},{1,13},{5,1},{9,5},{13,9},{2,14},{6,2},{... | collective-permute-start | bytes 1179656 | tf_op jit(solution)/shard_map/ppermute | solution.py:366
  6.8 0.0 collective-permute-start.2
  6.8 0.1 pad_add_fusion.where_ref
  6.9 18.5 %planes.1 = (f32[2,4,64,128]{3,2,1,0:T(8,128)S(1)}, f32[128,128]{1,0:T(8,128)S(1)}) custom-call(s32[4]{0:T(128)S(1)} %pad_add_fusion.where_ref, bf16[2,2,3,2048,128]{4,3,2,1,0:T(8,128)(2,1)} %v_ref.3, bf16[2,3,3,3,2,2048]{5,4,3,2,1,0:T(2,128)(2,1)} %bitcast.20, bf16[2,3,3,3,2,2048]{5,4,3,2,1,0:T(2,128)(2,1)} %bitcast.21), custom_call_target="tpu_custom_call" | custom-call | flops 20000000000 | bytes 4194304 | tf_op jit(solution)/shard_map/planes/pallas_call | solution.py:379
  25.4 0.0 copy-start.3
  25.4 0.0 copy-start
  25.4 0.0 copy-start.1
  25.4 0.0 copy-start.2
  25.4 0.1 collective-permute-start
  25.5 0.0 collective-permute-done.2
  25.5 0.0 collective-permute-done.1.halo_ref
  25.5 2.5 %rim.1 = f32[2,1,64,128]{3,2,1,0:T(8,128)S(1)} custom-call(s32[4]{0:T(128)S(1)} %pad_add_fusion.where_ref, bf16[2,2,3,2048,128]{4,3,2,1,0:T(8,128)(2,1)} %v_ref.3, bf16[2,3,256,128]{3,2,1,0:T(8,128)(2,1)S(1)} %collective-permute-done.1.halo_ref, bf16[2,3,3,3,2,2048]{5,4,3,2,1,0:T(2,128)(2,1)} %bitcast.22, f32[128,128]{1,0:T(8,128)S(1)} %get-tuple-element.14.inner_ref), custom_call_target="tpu_custom_call" | custom-call | flops 2000000000 | bytes 4194304 | tf_op jit(solution)/shard_map/rim/pallas_call | solution.py:420
  28.0 3.4 %collective-permute-done = f32[4,64,128]{2,1,0:T(8,128)S(1)} collective-permute-done((f32[4,64,128]{2,1,0:T(8,128)S(1)}, f32[4,64,128]{2,1,0:T(8,128)S(1)}, u32[]{:S(2)}, u32[]{:S(2)}) %collective-permute-start) | collective-permute-done | bytes 131104 | tf_op jit(solution)/shard_map/ppermute | solution.py:19
  31.4 0.1 collective-permute-start.3
  31.5 1.0 %collective-permute-start.4 = (f32[1,64,128]{2,1,0:T(8,128)S(1)}, f32[1,64,128]{2,1,0:T(8,128)S(1)}, u32[]{:S(2)}, u32[]{:S(2)}) collective-permute-start(f32[1,64,128]{2,1,0:T(8,128)S(1)} %get-tuple-element.24), channel_id=1, source_target_pairs={{0,4},{4,0},{8,12},{12,8},{1,5},{5,1},{9,13},{13,9},{2,6},{6,2},{1... | collective-permute-start | bytes 98312 | tf_op jit(solution)/shard_map/ppermute | solution.py:19
  32.5 3.0 %collective-permute-done.4 = f32[1,64,128]{2,1,0:T(8,128)S(1)} collective-permute-done((f32[1,64,128]{2,1,0:T(8,128)S(1)}, f32[1,64,128]{2,1,0:T(8,128)S(1)}, u32[]{:S(2)}, u32[]{:S(2)}) %collective-permute-start.4) | collective-permute-done | bytes 32800 | tf_op jit(solution)/shard_map/ppermute | solution.py:19
  35.5 3.3 %collective-permute-start.5 = (f32[1,64,128]{2,1,0:T(8,128)S(1)}, f32[1,64,128]{2,1,0:T(8,128)S(1)}, u32[]{:S(2)}, u32[]{:S(2)}) collective-permute-start(f32[1,64,128]{2,1,0:T(8,128)S(1)} %add.14.mine_b), channel_id=1, source_target_pairs={{0,8},{4,12},{8,0},{12,4},{1,9},{5,13},{9,1},{13,5},{2,10},{6,14},... | collective-permute-start | bytes 98312 | tf_op jit(solution)/shard_map/ppermute | solution.py:19
  38.8 2.5 %collective-permute-done.5.got_b = f32[1,64,128]{2,1,0:T(8,128)S(1)} collective-permute-done((f32[1,64,128]{2,1,0:T(8,128)S(1)}, f32[1,64,128]{2,1,0:T(8,128)S(1)}, u32[]{:S(2)}, u32[]{:S(2)}) %collective-permute-start.5) | collective-permute-done | bytes 32800 | tf_op jit(solution)/shard_map/ppermute | solution.py:19
  41.3 0.0 collective-permute-done.3.got_a
  41.3 1.2 %collective-permute-start.8 = (bf16[5,64,128]{2,1,0:T(8,128)(2,1)S(1)}, bf16[5,64,128]{2,1,0:T(8,128)(2,1)S(1)}, u32[]{:S(2)}, u32[]{:S(2)}) collective-permute-start(bf16[5,64,128]{2,1,0:T(8,128)(2,1)S(1)} %round.1.refs_0_), channel_id=1, source_target_pairs={{0,4},{2,6},{4,0},{6,2},{8,12},{10,14},{12,8},{14,10},{1,5},{3,7},... | collective-permute-start | bytes 245768 | tf_op jit(solution)/shard_map/ppermute | solution.py:27
  42.5 0.0 collective-permute-start.9
  42.5 1.5 %collective-permute-start.6 = (bf16[5,64,128]{2,1,0:T(8,128)(2,1)S(1)}, bf16[5,64,128]{2,1,0:T(8,128)(2,1)S(1)}, u32[]{:S(2)}, u32[]{:S(2)}) collective-permute-start(bf16[5,64,128]{2,1,0:T(8,128)(2,1)S(1)} %round.1.refs_0_), channel_id=1, source_target_pairs={{0,2},{2,0},{4,6},{6,4},{8,10},{10,8},{12,14},{14,12},{1,3},{3,1},... | collective-permute-start | bytes 245768 | tf_op jit(solution)/shard_map/ppermute | solution.py:27
  44.0 0.9 %collective-permute-start.7 = (bf16[5,64,128]{2,1,0:T(8,128)(2,1)S(1)}, bf16[5,64,128]{2,1,0:T(8,128)(2,1)S(1)}, u32[]{:S(2)}, u32[]{:S(2)}) collective-permute-start(bf16[5,64,128]{2,1,0:T(8,128)(2,1)S(1)} %round.1.refs_0_), channel_id=1, source_target_pairs={{0,6},{2,4},{4,2},{6,0},{8,14},{10,12},{12,10},{14,8},{1,7},{3,5},... | collective-permute-start | bytes 245768 | tf_op jit(solution)/shard_map/ppermute | solution.py:27
  44.9 0.9 %collective-permute-done.8.refs_1_ = bf16[5,64,128]{2,1,0:T(8,128)(2,1)S(1)} collective-permute-done((bf16[5,64,128]{2,1,0:T(8,128)(2,1)S(1)}, bf16[5,64,128]{2,1,0:T(8,128)(2,1)S(1)}, u32[]{:S(2)}, u32[]{:S(2)}) %collective-permute-start.8) | collective-permute-done | bytes 81952 | tf_op jit(solution)/shard_map/ppermute | solution.py:27
  45.8 0.0 collective-permute-start.10
  45.8 0.0 copy-done.3
  45.9 0.1 pad_add_fusion.1.codes_ref
  45.9 0.0 collective-permute-done.9.refs_2_.refs_4_
  45.9 1.2 %collective-permute-done.10.refs_3_.refs_5_ = bf16[5,64,128]{2,1,0:T(8,128)(2,1)S(1)} collective-permute-done((bf16[5,64,128]{2,1,0:T(8,128)(2,1)S(1)}, bf16[5,64,128]{2,1,0:T(8,128)(2,1)S(1)}, u32[]{:S(2)}, u32[]{:S(2)}) %collective-permute-start.10) | collective-permute-done | bytes 81952 | tf_op jit(solution)/shard_map/ppermute | solution.py:19
  47.1 1.5 %rows.1 = f32[2,2,32,2,128]{4,3,2,1,0:T(2,128)} custom-call(s32[4]{0:T(128)S(1)} %pad_add_fusion.where_ref, s32[4]{0:T(128)S(1)} %pad_add_fusion.1.codes_ref, bf16[5,64,128]{2,1,0:T(8,128)(2,1)S(1)} %round.1.refs_0_, bf16[5,64,128]{2,1,0:T(8,128)(2,1)S(1)} %collective-permute-done.8.refs_1_, bf16[5,64,128]{2,1,0:T(8,128)(2,1)S(1)} %collective-permute-done.9.refs_2_.refs_4_, ...), custom_call_target="tpu_custom_call" | custom-call | tf_op jit(solution)/shard_map/rows/pallas_call | solution.py:469
  48.6 0.0 collective-permute-done.6.refs_2_
  48.6 0.9 %collective-permute-done.7.refs_3_ = bf16[5,64,128]{2,1,0:T(8,128)(2,1)S(1)} collective-permute-done((bf16[5,64,128]{2,1,0:T(8,128)(2,1)S(1)}, bf16[5,64,128]{2,1,0:T(8,128)(2,1)S(1)}, u32[]{:S(2)}, u32[]{:S(2)}) %collective-permute-start.7) | collective-permute-done | bytes 81952 | tf_op jit(solution)/shard_map/ppermute | solution.py:27
  49.5 0.0 collective-permute-start.11
  49.5 0.5 collective-permute-start.12
  50.0 0.8 %collective-permute-done.11.refs_6_ = bf16[5,64,128]{2,1,0:T(8,128)(2,1)S(1)} collective-permute-done((bf16[5,64,128]{2,1,0:T(8,128)(2,1)S(1)}, bf16[5,64,128]{2,1,0:T(8,128)(2,1)S(1)}, u32[]{:S(2)}, u32[]{:S(2)}) %collective-permute-start.11) | collective-permute-done | bytes 81952 | tf_op jit(solution)/shard_map/ppermute | solution.py:19
  50.7 0.2 collective-permute-done.12.refs_7_
  50.9 0.0 copy-done
  50.9 0.0 copy-done.1
  50.9 0.0 copy-done.2
  50.9 4.9 %pairs.1 = f32[2,4]{1,0:T(2,128)S(1)} custom-call(s32[4]{0:T(128)S(1)} %pad_add_fusion.where_ref, s32[4]{0:T(128)S(1)} %pad_add_fusion.1.codes_ref, s32[2,4]{1,0:T(2,128)S(1)} %bitcast.18, s32[2,4]{1,0:T(2,128)S(1)} %bitcast.19, bf16[5,64,128]{2,1,0:T(8,128)(2,1)S(1)} %round.1.refs_0_, bf16[5,64,128]{2,1,0:T(8,128)(2,1)S(1)} %collective-permute-done.8.refs_1_, ...), custom_call_target="tpu_custom_call" | custom-call | tf_op jit(solution)/shard_map/pairs/pallas_call | solution.py:489
  55.8 0.4 collective-permute-start.13
  56.3 0.8 %collective-permute-done.13 = f32[2,4]{1,0:T(2,128)S(1)} collective-permute-done((f32[2,4]{1,0:T(2,128)S(1)}, f32[2,4]{1,0:T(2,128)S(1)}, u32[]{:S(2)}, u32[]{:S(2)}) %collective-permute-start.13) | collective-permute-done | bytes 64 | tf_op jit(solution)/shard_map/ppermute | solution.py:19
  57.1 0.6 add_bitcast_fusion
  (5 shorter events, 0.1 us)
Async XLA Ops:
  1.7 23.9 %collective-permute-start.1 = (bf16[2,3,256,128]{3,2,1,0:T(8,128)(2,1)S(1)}, bf16[2,3,256,128]{3,2,1,0:T(8,128)(2,1)S(1)}, u32[]{:S(2)}, u32[]{:S(2)}) collective-permute-start(bf16[2,3,256,128]{3,2,1,0:T(8,128)(2,1)S(1)} %dynamic-slice_bitcast_fusion), channel_id=1, source_target_pairs={{0,12},{4,0},{8,4},{12,8},{1,13},{5,1},{9,5},{13,9},{2,14},{6,2},{... | collective-permute-start | bytes 1179656 | tf_op jit(solution)/shard_map/ppermute | solution.py:366
  6.8 18.7 %collective-permute-start.2 = (s32[2]{0:T(128)}, s32[2]{0:T(128)S(1)}, u32[]{:S(2)}, u32[]{:S(2)}) collective-permute-start(s32[2]{0:T(128)} %param.8), channel_id=1, source_target_pairs={{0,1},{1,0},{2,3},{3,2},{4,5},{5,4},{6,7},{7,6},{8,9},{9,8},{10,11... | collective-permute-start | bytes 32 | tf_op jit(solution)/shard_map/ppermute | solution.py:19
  25.4 20.5 %copy-start.3 = (s32[2]{0:T(128)S(1)}, s32[2]{0:T(128)}, u32[]{:S(2)}) copy-start(s32[2]{0:T(128)} %param.8) | copy-start | bytes 28
  25.4 25.5 %copy-start = (bf16[4,8,2,128,128]{4,3,2,1,0:T(8,128)(2,1)S(1)}, bf16[4,8,2,128,128]{4,3,2,1,0:T(8,128)(2,1)}, u32[]{:S(2)}) copy-start(bf16[4,8,2,128,128]{4,3,2,1,0:T(8,128)(2,1)} %refs_8_.1) | copy-start | bytes 6291460
  25.4 25.5 %copy-start.1 = (s32[4,2]{0,1:T(2,128)S(1)}, s32[4,2]{0,1:T(2,128)}, u32[]{:S(2)}) copy-start(s32[4,2]{0,1:T(2,128)} %param.9) | copy-start | bytes 100
  25.4 25.5 %copy-start.2 = (s32[4,2]{0,1:T(2,128)S(1)}, s32[4,2]{0,1:T(2,128)}, u32[]{:S(2)}) copy-start(s32[4,2]{0,1:T(2,128)} %param.10) | copy-start | bytes 100
  25.4 6.0 %collective-permute-start = (f32[4,64,128]{2,1,0:T(8,128)S(1)}, f32[4,64,128]{2,1,0:T(8,128)S(1)}, u32[]{:S(2)}, u32[]{:S(2)}) collective-permute-start(f32[4,64,128]{2,1,0:T(8,128)S(1)} %get-tuple-element.22), channel_id=1, source_target_pairs={{0,4},{4,0},{8,12},{12,8},{1,5},{5,1},{9,13},{13,9},{2,6},{6,2},{1... | collective-permute-start | bytes 393224 | tf_op jit(solution)/shard_map/ppermute | solution.py:19
  31.4 9.9 %collective-permute-start.3 = (f32[4,64,128]{2,1,0:T(8,128)S(1)}, f32[4,64,128]{2,1,0:T(8,128)S(1)}, u32[]{:S(2)}, u32[]{:S(2)}) collective-permute-start(f32[4,64,128]{2,1,0:T(8,128)S(1)} %add.13.mine_a), channel_id=1, source_target_pairs={{0,8},{4,12},{8,0},{12,4},{1,9},{5,13},{9,1},{13,5},{2,10},{6,14},... | collective-permute-start | bytes 393224 | tf_op jit(solution)/shard_map/ppermute | solution.py:19
  31.5 4.0 %collective-permute-start.4 = (f32[1,64,128]{2,1,0:T(8,128)S(1)}, f32[1,64,128]{2,1,0:T(8,128)S(1)}, u32[]{:S(2)}, u32[]{:S(2)}) collective-permute-start(f32[1,64,128]{2,1,0:T(8,128)S(1)} %get-tuple-element.24), channel_id=1, source_target_pairs={{0,4},{4,0},{8,12},{12,8},{1,5},{5,1},{9,13},{13,9},{2,6},{6,2},{1... | collective-permute-start | bytes 98312 | tf_op jit(solution)/shard_map/ppermute | solution.py:19
  35.5 5.8 %collective-permute-start.5 = (f32[1,64,128]{2,1,0:T(8,128)S(1)}, f32[1,64,128]{2,1,0:T(8,128)S(1)}, u32[]{:S(2)}, u32[]{:S(2)}) collective-permute-start(f32[1,64,128]{2,1,0:T(8,128)S(1)} %add.14.mine_b), channel_id=1, source_target_pairs={{0,8},{4,12},{8,0},{12,4},{1,9},{5,13},{9,1},{13,5},{2,10},{6,14},... | collective-permute-start | bytes 98312 | tf_op jit(solution)/shard_map/ppermute | solution.py:19
  41.3 4.5 %collective-permute-start.8 = (bf16[5,64,128]{2,1,0:T(8,128)(2,1)S(1)}, bf16[5,64,128]{2,1,0:T(8,128)(2,1)S(1)}, u32[]{:S(2)}, u32[]{:S(2)}) collective-permute-start(bf16[5,64,128]{2,1,0:T(8,128)(2,1)S(1)} %round.1.refs_0_), channel_id=1, source_target_pairs={{0,4},{2,6},{4,0},{6,2},{8,12},{10,14},{12,8},{14,10},{1,5},{3,7},... | collective-permute-start | bytes 245768 | tf_op jit(solution)/shard_map/ppermute | solution.py:27
  42.5 3.4 %collective-permute-start.9 = (bf16[5,64,128]{2,1,0:T(8,128)(2,1)S(1)}, bf16[5,64,128]{2,1,0:T(8,128)(2,1)S(1)}, u32[]{:S(2)}, u32[]{:S(2)}) collective-permute-start(bf16[5,64,128]{2,1,0:T(8,128)(2,1)S(1)} %round.1.refs_0_), channel_id=1, source_target_pairs={{0,1},{1,0},{2,3},{3,2},{4,5},{5,4},{6,7},{7,6},{8,9},{9,8},{10,11... | collective-permute-start | bytes 245768 | tf_op jit(solution)/shard_map/ppermute | solution.py:19
  42.5 6.1 %collective-permute-start.6 = (bf16[5,64,128]{2,1,0:T(8,128)(2,1)S(1)}, bf16[5,64,128]{2,1,0:T(8,128)(2,1)S(1)}, u32[]{:S(2)}, u32[]{:S(2)}) collective-permute-start(bf16[5,64,128]{2,1,0:T(8,128)(2,1)S(1)} %round.1.refs_0_), channel_id=1, source_target_pairs={{0,2},{2,0},{4,6},{6,4},{8,10},{10,8},{12,14},{14,12},{1,3},{3,1},... | collective-permute-start | bytes 245768 | tf_op jit(solution)/shard_map/ppermute | solution.py:27
  44.0 5.5 %collective-permute-start.7 = (bf16[5,64,128]{2,1,0:T(8,128)(2,1)S(1)}, bf16[5,64,128]{2,1,0:T(8,128)(2,1)S(1)}, u32[]{:S(2)}, u32[]{:S(2)}) collective-permute-start(bf16[5,64,128]{2,1,0:T(8,128)(2,1)S(1)} %round.1.refs_0_), channel_id=1, source_target_pairs={{0,6},{2,4},{4,2},{6,0},{8,14},{10,12},{12,10},{14,8},{1,7},{3,5},... | collective-permute-start | bytes 245768 | tf_op jit(solution)/shard_map/ppermute | solution.py:27
  45.8 1.3 %collective-permute-start.10 = (bf16[5,64,128]{2,1,0:T(8,128)(2,1)S(1)}, bf16[5,64,128]{2,1,0:T(8,128)(2,1)S(1)}, u32[]{:S(2)}, u32[]{:S(2)}) collective-permute-start(bf16[5,64,128]{2,1,0:T(8,128)(2,1)S(1)} %collective-permute-done.8.refs_1_), channel_id=1, source_target_pairs={{0,1},{1,0},{2,3},{3,2},{4,5},{5,4},{6,7},{7,6},{8,9},{9,8},{10,11... | collective-permute-start | bytes 245768 | tf_op jit(solution)/shard_map/ppermute | solution.py:19
  49.5 1.3 %collective-permute-start.11 = (bf16[5,64,128]{2,1,0:T(8,128)(2,1)S(1)}, bf16[5,64,128]{2,1,0:T(8,128)(2,1)S(1)}, u32[]{:S(2)}, u32[]{:S(2)}) collective-permute-start(bf16[5,64,128]{2,1,0:T(8,128)(2,1)S(1)} %collective-permute-done.6.refs_2_), channel_id=1, source_target_pairs={{0,1},{1,0},{2,3},{3,2},{4,5},{5,4},{6,7},{7,6},{8,9},{9,8},{10,11... | collective-permute-start | bytes 245768 | tf_op jit(solution)/shard_map/ppermute | solution.py:19
  49.5 1.4 %collective-permute-start.12 = (bf16[5,64,128]{2,1,0:T(8,128)(2,1)S(1)}, bf16[5,64,128]{2,1,0:T(8,128)(2,1)S(1)}, u32[]{:S(2)}, u32[]{:S(2)}) collective-permute-start(bf16[5,64,128]{2,1,0:T(8,128)(2,1)S(1)} %collective-permute-done.7.refs_3_), channel_id=1, source_target_pairs={{0,1},{1,0},{2,3},{3,2},{4,5},{5,4},{6,7},{7,6},{8,9},{9,8},{10,11... | collective-permute-start | bytes 245768 | tf_op jit(solution)/shard_map/ppermute | solution.py:19
  55.8 1.2 %collective-permute-start.13 = (f32[2,4]{1,0:T(2,128)S(1)}, f32[2,4]{1,0:T(2,128)S(1)}, u32[]{:S(2)}, u32[]{:S(2)}) collective-permute-start(f32[2,4]{1,0:T(2,128)S(1)} %pairs.1), channel_id=1, source_target_pairs={{0,1},{1,0},{2,3},{3,2},{4,5},{5,4},{6,7},{7,6},{8,9},{9,8},{10,11... | collective-permute-start | bytes 104 | tf_op jit(solution)/shard_map/ppermute | solution.py:19
